TPU v7x, 128 devices: a whole 4x4x4 slice. The times are simulated.
128 devices in a mesh: layer: 32 (over y, x, core), dp: 4 (over z).
Axes of the slice: x: 4, y: 4, z: 4, core: 2. Of those that a mesh axis runs over, the one named last changes fastest.
Arguments:
- inputs: float32 [512, 1024], P('dp'), may hold values from -6 to 6
- guesses: float32 [32, 512, 1024], P('layer', 'dp'), may hold values from -6 to 6
- weights: bfloat16 [128, 1024, 1024], P('layer'), may hold values from -0.1875 to 0.1875
- biases: float32 [128, 1024], P('layer'), may hold values from -3 to 3
- adjoint: bfloat16 [32, 512, 1024], P('layer', 'dp'), may hold values from -6 to 6
Outputs:
- new_states: float32 [32, 512, 1024], P('layer', 'dp')
- coarse_states: float32 [32, 512, 1024], P('layer', 'dp')
- weight_grad: float32 [32, 1024, 1024], P('layer', None, 'dp')
All inputs are finite; a program needn't handle non-finite values.
Results may differ from a plain program's by a relative error of at most 0.007.
Values may be sent and summed in bfloat16 or wider, within the bound.
A program may use at most 64 MiB of HBM per device.

v0:
```python
import jax
import jax.numpy as jnp
from jax import lax
from jax.sharding import PartitionSpec as P


def passed_along(shard, axis, by):
    devices = lax.axis_size(axis)
    pairs = [(i, i + by) for i in range(devices) if 0 <= i + by < devices]
    return lax.ppermute(shard, axis, pairs)


def laid_out(tiles, dim):
    shape = list(tiles.shape[1:])
    shape[dim] *= tiles.shape[0]
    return jnp.moveaxis(tiles, 0, dim).reshape(shape)


def sent_to_all(shard, axis):
    devices = lax.axis_size(axis)
    return lax.all_to_all(
        jnp.broadcast_to(shard[None], (devices, *shard.shape)), axis, 0, 0, tiled=True
    )


def gather_directly(shard, axis, dim):
    return laid_out(sent_to_all(shard, axis), dim)


def advance(layer_state, weight, bias_row, step_size):
    pre_tanh = (
        jnp.dot(layer_state.astype(jnp.bfloat16), weight, preferred_element_type=jnp.float32)
        + bias_row
    )
    return (layer_state + step_size * jnp.tanh(pre_tanh), pre_tanh)


def body(inputs, guesses, weights, biases, adjoint):
    blocks = lax.axis_size("layer")
    step_size = 4.0 / (4 * blocks)
    device_idx = lax.axis_index("layer")
    position = (device_idx + 1) % 4
    is_first = device_idx == 0
    is_early = device_idx < 4

    def fine_block(start):
        current = start
        last_in = start
        pre_tanh = start
        for layer_idx in range(4):
            if layer_idx == 3:
                last_in = current
            current, pre_tanh = advance(current, weights[layer_idx], biases[layer_idx], step_size)
        return (current, last_in, pre_tanh)

    def coarse_step(layer_state, factor):
        return advance(layer_state, weights[0], biases[0], factor * step_size)[0]

    guess_prev = jnp.where(is_first, inputs, passed_along(guesses[0], "layer", 1))
    relaxed = fine_block(guess_prev)[0]
    relaxed_prev = jnp.where(is_first, inputs, passed_along(relaxed, "layer", 1))
    ahead = fine_block(relaxed_prev)[0]
    forcing = ahead - coarse_step(relaxed_prev, 4.0)

    def level_round(current):
        received = passed_along(current, "layer", 1)
        return coarse_step(jnp.where(is_first, inputs, received), 4.0) + forcing

    current = relaxed
    for target in (1, 2, 3, 0, 1, 2, 3):
        current = jnp.where(position == target, level_round(current), current)
    update = level_round(current)
    below = jnp.where(is_early, inputs, passed_along(current, "layer", 4))
    coarse_force = update - coarse_step(below, 16.0)

    def coarse_chain(turn, carried):
        received = passed_along(carried, "layer", 4)
        return coarse_step(jnp.where(is_early, inputs, received), 16.0) + coarse_force

    solved = lax.fori_loop(0, blocks // 4, coarse_chain, current)
    coarse_states = solved - relaxed
    current = jnp.where(position == 0, solved, current)
    for target in (1, 2, 3):
        current = jnp.where(position == target, level_round(current), current)
    final_prev = jnp.where(is_first, inputs, passed_along(current, "layer", 1))
    new_states, last_in, pre_tanh = fine_block(final_prev)
    tanh_val = jnp.tanh(pre_tanh)
    deltas = (adjoint[0].astype(jnp.float32) * step_size * (1.0 - tanh_val * tanh_val)).astype(
        jnp.bfloat16
    )
    left_rows = last_in.astype(jnp.bfloat16)
    all_rows = gather_directly(left_rows, "dp", 0)
    own_deltas = lax.all_to_all(deltas, "dp", split_axis=1, concat_axis=0, tiled=True)
    weight_grad = jnp.einsum("rd,re->de", all_rows, own_deltas, preferred_element_type=jnp.float32)
    return (new_states[None], coarse_states[None], weight_grad[None])


def solution(mesh):
    return jax.shard_map(
        body,
        mesh=mesh,
        in_specs=(
            P("dp", None),
            P("layer", "dp", None),
            P("layer", None, None),
            P("layer", None),
            P("layer", "dp", None),
        ),
        out_specs=(P("layer", "dp", None), P("layer", "dp", None), P("layer", None, "dp")),
        check_vma=False,
    )
```

profile of v0, /device:TPU:16, one launch (start us, length us, event | category | flops | bytes accessed | tf_op | source)
XLA Modules:
  0.0 388.3 jit_solution(7435857109970388201)
XLA Ops:
  3.6 10.0 %collective-permute-done.1 = f32[128,1024]{1,0:T(8,128)S(1)} collective-permute-done((f32[128,1024]{1,0:T(8,128)}, f32[128,1024]{1,0:T(8,128)S(1)}, u32[]{:S(2)}, u32[]{:S(2)}) %collective-permute-start.1) | collective-permute-done | bytes 524320 | tf_op jit(solution)/shard_map/ppermute | solution.py:10
  13.6 2.2 fusion.85
  23.9 10.7 %collective-permute-done.2 = f32[128,1024]{1,0:T(8,128)S(1)} collective-permute-done((f32[128,1024]{1,0:T(8,128)S(1)}, f32[128,1024]{1,0:T(8,128)S(1)}, u32[]{:S(2)}, u32[]{:S(2)}) %collective-permute-start.2) | collective-permute-done | bytes 524320 | tf_op jit(solution)/shard_map/ppermute | solution.py:10
  36.7 2.1 fusion.319
  41.0 2.2 add_select_fusion
  45.1 10.7 %collective-permute-done.3 = f32[128,1024]{1,0:T(8,128)S(1)} collective-permute-done((f32[128,1024]{1,0:T(8,128)S(1)}, f32[128,1024]{1,0:T(8,128)S(1)}, u32[]{:S(2)}, u32[]{:S(2)}) %collective-permute-start.3) | collective-permute-done | bytes 524320 | tf_op jit(solution)/shard_map/ppermute | solution.py:10
  59.8 10.7 %collective-permute-done.4 = f32[128,1024]{1,0:T(8,128)S(1)} collective-permute-done((f32[128,1024]{1,0:T(8,128)S(1)}, f32[128,1024]{1,0:T(8,128)S(1)}, u32[]{:S(2)}, u32[]{:S(2)}) %collective-permute-start.4) | collective-permute-done | bytes 524320 | tf_op jit(solution)/shard_map/ppermute | solution.py:10
  74.5 10.7 %collective-permute-done.5 = f32[128,1024]{1,0:T(8,128)S(1)} collective-permute-done((f32[128,1024]{1,0:T(8,128)S(1)}, f32[128,1024]{1,0:T(8,128)S(1)}, u32[]{:S(2)}, u32[]{:S(2)}) %collective-permute-start.5) | collective-permute-done | bytes 524320 | tf_op jit(solution)/shard_map/ppermute | solution.py:10
  89.2 10.7 %collective-permute-done.6 = f32[128,1024]{1,0:T(8,128)S(1)} collective-permute-done((f32[128,1024]{1,0:T(8,128)S(1)}, f32[128,1024]{1,0:T(8,128)S(1)}, u32[]{:S(2)}, u32[]{:S(2)}) %collective-permute-start.6) | collective-permute-done | bytes 524320 | tf_op jit(solution)/shard_map/ppermute | solution.py:10
  99.8 2.1 fusion.163
  103.9 10.7 %collective-permute-done.7 = f32[128,1024]{1,0:T(8,128)S(1)} collective-permute-done((f32[128,1024]{1,0:T(8,128)S(1)}, f32[128,1024]{1,0:T(8,128)S(1)}, u32[]{:S(2)}, u32[]{:S(2)}) %collective-permute-start.7) | collective-permute-done | bytes 524320 | tf_op jit(solution)/shard_map/ppermute | solution.py:10
  114.6 2.1 fusion.181
  118.7 10.7 %collective-permute-done.8 = f32[128,1024]{1,0:T(8,128)S(1)} collective-permute-done((f32[128,1024]{1,0:T(8,128)S(1)}, f32[128,1024]{1,0:T(8,128)S(1)}, u32[]{:S(2)}, u32[]{:S(2)}) %collective-permute-start.8) | collective-permute-done | bytes 524320 | tf_op jit(solution)/shard_map/ppermute | solution.py:10
  129.4 2.1 fusion.199
  136.2 10.4 %collective-permute-done.10 = f32[128,1024]{1,0:T(8,128)S(1)} collective-permute-done((f32[128,1024]{1,0:T(8,128)S(1)}, f32[128,1024]{1,0:T(8,128)S(1)}, u32[]{:S(2)}, u32[]{:S(2)}) %collective-permute-start.10) | collective-permute-done | bytes 524320 | tf_op jit(solution)/shard_map/ppermute | solution.py:10
  148.6 8.1 %collective-permute-done.9 = f32[128,1024]{1,0:T(8,128)S(1)} collective-permute-done((f32[128,1024]{1,0:T(8,128)S(1)}, f32[128,1024]{1,0:T(8,128)S(1)}, u32[]{:S(2)}, u32[]{:S(2)}) %collective-permute-start.9) | collective-permute-done | bytes 524320 | tf_op jit(solution)/shard_map/ppermute | solution.py:10
  158.9 140.0 %while.10 = (s32[]{:T(128)}, f32[128,1024]{1,0:T(8,128)}, pred[]{:T(512)}, f32[128,1024]{1,0:T(8,128)S(1)}, bf16[4,1024,1024]{2,1,0:T(8,128)(2,1)}, /*index=5*/f...) while((s32[]{:T(128)}, f32[128,1024]{1,0:T(8,128)}, pred[]{:T(512)}, f32[128,1024]{1,0:T(8,128)S(1)}, ...), condition=%wide.region_1.2_spmd, body=%wide.region_0.1_spmd.sunk | while | flops 269352960 | bytes 7353469 | solution.py:80
  158.9 2.2 collective-permute-start
  161.8 12.1 %collective-permute-done = f32[128,1024]{1,0:T(8,128)S(1)} collective-permute-done((f32[128,1024]{1,0:T(8,128)}, f32[128,1024]{1,0:T(8,128)S(1)}, u32[]{:S(2)}, u32[]{:S(2)}) %collective-permute-start) | collective-permute-done | bytes 524320 | tf_op jit(solution)/shard_map/while/body/eval_jaxpr/ppermute | solution.py:10
  174.0 2.9 fusion.480
  176.9 3.9 %collective-permute-start = (f32[128,1024]{1,0:T(8,128)}, f32[128,1024]{1,0:T(8,128)S(1)}, u32[]{:S(2)}, u32[]{:S(2)}) collective-permute-start(f32[128,1024]{1,0:T(8,128)} %get-tuple-element.119), channel_id=1, source_target_pairs={{0,16},{4,20},{8,24},{12,28},{16,32},{20,36},{24,40},{28,44},{32,4... | collective-permute-start | bytes 1572872 | tf_op jit(solution)/shard_map/while/body/eval_jaxpr/ppermute | solution.py:10
  181.5 10.5 %collective-permute-done = f32[128,1024]{1,0:T(8,128)S(1)} collective-permute-done((f32[128,1024]{1,0:T(8,128)}, f32[128,1024]{1,0:T(8,128)S(1)}, u32[]{:S(2)}, u32[]{:S(2)}) %collective-permute-start) | collective-permute-done | bytes 524320 | tf_op jit(solution)/shard_map/while/body/eval_jaxpr/ppermute | solution.py:10
  192.0 2.9 fusion.480
  194.9 4.7 %collective-permute-start = (f32[128,1024]{1,0:T(8,128)}, f32[128,1024]{1,0:T(8,128)S(1)}, u32[]{:S(2)}, u32[]{:S(2)}) collective-permute-start(f32[128,1024]{1,0:T(8,128)} %get-tuple-element.119), channel_id=1, source_target_pairs={{0,16},{4,20},{8,24},{12,28},{16,32},{20,36},{24,40},{28,44},{32,4... | collective-permute-start | bytes 1572872 | tf_op jit(solution)/shard_map/while/body/eval_jaxpr/ppermute | solution.py:10
  200.3 9.9 %collective-permute-done = f32[128,1024]{1,0:T(8,128)S(1)} collective-permute-done((f32[128,1024]{1,0:T(8,128)}, f32[128,1024]{1,0:T(8,128)S(1)}, u32[]{:S(2)}, u32[]{:S(2)}) %collective-permute-start) | collective-permute-done | bytes 524320 | tf_op jit(solution)/shard_map/while/body/eval_jaxpr/ppermute | solution.py:10
  210.2 2.9 fusion.480
  213.1 4.4 %collective-permute-start = (f32[128,1024]{1,0:T(8,128)}, f32[128,1024]{1,0:T(8,128)S(1)}, u32[]{:S(2)}, u32[]{:S(2)}) collective-permute-start(f32[128,1024]{1,0:T(8,128)} %get-tuple-element.119), channel_id=1, source_target_pairs={{0,16},{4,20},{8,24},{12,28},{16,32},{20,36},{24,40},{28,44},{32,4... | collective-permute-start | bytes 1572872 | tf_op jit(solution)/shard_map/while/body/eval_jaxpr/ppermute | solution.py:10
  218.2 9.4 %collective-permute-done = f32[128,1024]{1,0:T(8,128)S(1)} collective-permute-done((f32[128,1024]{1,0:T(8,128)}, f32[128,1024]{1,0:T(8,128)S(1)}, u32[]{:S(2)}, u32[]{:S(2)}) %collective-permute-start) | collective-permute-done | bytes 524320 | tf_op jit(solution)/shard_map/while/body/eval_jaxpr/ppermute | solution.py:10
  227.6 2.9 fusion.480
  230.4 4.1 %collective-permute-start = (f32[128,1024]{1,0:T(8,128)}, f32[128,1024]{1,0:T(8,128)S(1)}, u32[]{:S(2)}, u32[]{:S(2)}) collective-permute-start(f32[128,1024]{1,0:T(8,128)} %get-tuple-element.119), channel_id=1, source_target_pairs={{0,16},{4,20},{8,24},{12,28},{16,32},{20,36},{24,40},{28,44},{32,4... | collective-permute-start | bytes 1572872 | tf_op jit(solution)/shard_map/while/body/eval_jaxpr/ppermute | solution.py:10
  235.3 8.9 %collective-permute-done = f32[128,1024]{1,0:T(8,128)S(1)} collective-permute-done((f32[128,1024]{1,0:T(8,128)}, f32[128,1024]{1,0:T(8,128)S(1)}, u32[]{:S(2)}, u32[]{:S(2)}) %collective-permute-start) | collective-permute-done | bytes 524320 | tf_op jit(solution)/shard_map/while/body/eval_jaxpr/ppermute | solution.py:10
  244.1 2.9 fusion.480
  247.0 3.7 collective-permute-start
  251.5 9.2 %collective-permute-done = f32[128,1024]{1,0:T(8,128)S(1)} collective-permute-done((f32[128,1024]{1,0:T(8,128)}, f32[128,1024]{1,0:T(8,128)S(1)}, u32[]{:S(2)}, u32[]{:S(2)}) %collective-permute-start) | collective-permute-done | bytes 524320 | tf_op jit(solution)/shard_map/while/body/eval_jaxpr/ppermute | solution.py:10
  260.7 2.9 fusion.480
  263.6 2.8 collective-permute-start
  267.1 10.1 %collective-permute-done = f32[128,1024]{1,0:T(8,128)S(1)} collective-permute-done((f32[128,1024]{1,0:T(8,128)}, f32[128,1024]{1,0:T(8,128)S(1)}, u32[]{:S(2)}, u32[]{:S(2)}) %collective-permute-start) | collective-permute-done | bytes 524320 | tf_op jit(solution)/shard_map/while/body/eval_jaxpr/ppermute | solution.py:10
  277.3 2.9 fusion.480
  282.8 13.2 %collective-permute-done = f32[128,1024]{1,0:T(8,128)S(1)} collective-permute-done((f32[128,1024]{1,0:T(8,128)}, f32[128,1024]{1,0:T(8,128)S(1)}, u32[]{:S(2)}, u32[]{:S(2)}) %collective-permute-start) | collective-permute-done | bytes 524320 | tf_op jit(solution)/shard_map/while/body/eval_jaxpr/ppermute | solution.py:10
  296.0 2.9 fusion.480
  303.0 10.7 %collective-permute-done.11 = f32[128,1024]{1,0:T(8,128)S(1)} collective-permute-done((f32[128,1024]{1,0:T(8,128)S(1)}, f32[128,1024]{1,0:T(8,128)S(1)}, u32[]{:S(2)}, u32[]{:S(2)}) %collective-permute-start.11) | collective-permute-done | bytes 524320 | tf_op jit(solution)/shard_map/ppermute | solution.py:10
  317.7 10.7 %collective-permute-done.12 = f32[128,1024]{1,0:T(8,128)S(1)} collective-permute-done((f32[128,1024]{1,0:T(8,128)S(1)}, f32[128,1024]{1,0:T(8,128)S(1)}, u32[]{:S(2)}, u32[]{:S(2)}) %collective-permute-start.12) | collective-permute-done | bytes 524320 | tf_op jit(solution)/shard_map/ppermute | solution.py:10
  328.4 2.1 fusion.265
  332.6 10.7 %collective-permute-done.13 = f32[128,1024]{1,0:T(8,128)S(1)} collective-permute-done((f32[128,1024]{1,0:T(8,128)S(1)}, f32[128,1024]{1,0:T(8,128)S(1)}, u32[]{:S(2)}, u32[]{:S(2)}) %collective-permute-start.13) | collective-permute-done | bytes 524320 | tf_op jit(solution)/shard_map/ppermute | solution.py:10
  346.0 10.5 %collective-permute-done.14 = f32[128,1024]{1,0:T(8,128)S(1)} collective-permute-done((f32[128,1024]{1,0:T(8,128)S(1)}, f32[128,1024]{1,0:T(8,128)S(1)}, u32[]{:S(2)}, u32[]{:S(2)}) %collective-permute-start.14) | collective-permute-done | bytes 524320 | tf_op jit(solution)/shard_map/ppermute | solution.py:10
  360.0 5.3 %all-to-all-start.1 = ((bf16[128,4,256]{2,0,1:T(8,128)(2,1)}), bf16[128,4,256]{2,0,1:T(8,128)(2,1)S(1)}, u32[]{:S(2)}, u32[]{:S(2)}) async-start(bf16[128,4,256]{2,0,1:T(8,128)(2,1)} %bitcast.312), calls=%async_computation.1 | async-start | bytes 524288 | tf_op jit(solution)/shard_map/all_to_all | solution.py:93
  365.5 7.9 %all-to-all-done.1 = bf16[128,4,256]{2,0,1:T(8,128)(2,1)S(1)} async-done(((bf16[128,4,256]{2,0,1:T(8,128)(2,1)}), bf16[128,4,256]{2,0,1:T(8,128)(2,1)S(1)}, u32[]{:S(2)}, u32[]{:S(2)}) %all-to-all-start.1) | async-done | bytes 262176 | tf_op jit(solution)/shard_map/all_to_all | solution.py:93
  373.6 13.3 %all_to_all.21 = bf16[4,128,1024]{1,2,0:T(8,128)(2,1)S(1)} all-to-all(bf16[4,128,1024]{1,2,0:T(8,128)(2,1)S(1)} %broadcast_in_dim.17), channel_id=1, replica_groups=mesh['layer'=32,'dp'=4] {'dp'}, dimensions={0} | all-to-all | bytes 2097152 | tf_op jit(solution)/shard_map/all_to_all | solution.py:21
  (53 shorter events, 67.7 us)
Async XLA Ops:
  0.6 34.0 %copy-start.1 = (f32[128,1024]{1,0:T(8,128)S(1)}, f32[128,1024]{1,0:T(8,128)}, u32[]{:S(2)}) copy-start(f32[128,1024]{1,0:T(8,128)} %param.7) | copy-start | bytes 1572868
  0.6 13.0 %collective-permute-start.1 = (f32[128,1024]{1,0:T(8,128)}, f32[128,1024]{1,0:T(8,128)S(1)}, u32[]{:S(2)}, u32[]{:S(2)}) collective-permute-start(f32[128,1024]{1,0:T(8,128)} %bitcast.342), channel_id=1, source_target_pairs={{0,4},{4,8},{8,12},{12,16},{16,20},{20,24},{24,28},{28,32},{32,36}... | collective-permute-start | bytes 1572872 | tf_op jit(solution)/shard_map/ppermute | solution.py:10
  22.0 12.6 %collective-permute-start.2 = (f32[128,1024]{1,0:T(8,128)S(1)}, f32[128,1024]{1,0:T(8,128)S(1)}, u32[]{:S(2)}, u32[]{:S(2)}) collective-permute-start(f32[128,1024]{1,0:T(8,128)S(1)} %fusion.379), channel_id=1, source_target_pairs={{0,4},{4,8},{8,12},{12,16},{16,20},{20,24},{24,28},{28,32},{32,36}... | collective-permute-start | bytes 1572872 | tf_op jit(solution)/shard_map/ppermute | solution.py:10
  43.1 12.6 %collective-permute-start.3 = (f32[128,1024]{1,0:T(8,128)S(1)}, f32[128,1024]{1,0:T(8,128)S(1)}, u32[]{:S(2)}, u32[]{:S(2)}) collective-permute-start(f32[128,1024]{1,0:T(8,128)S(1)} %get-tuple-element.63), channel_id=1, source_target_pairs={{0,4},{4,8},{8,12},{12,16},{16,20},{20,24},{24,28},{28,32},{32,36}... | collective-permute-start | bytes 1572872 | tf_op jit(solution)/shard_map/ppermute | solution.py:10
  57.8 12.6 %collective-permute-start.4 = (f32[128,1024]{1,0:T(8,128)S(1)}, f32[128,1024]{1,0:T(8,128)S(1)}, u32[]{:S(2)}, u32[]{:S(2)}) collective-permute-start(f32[128,1024]{1,0:T(8,128)S(1)} %fusion.109), channel_id=1, source_target_pairs={{0,4},{4,8},{8,12},{12,16},{16,20},{20,24},{24,28},{28,32},{32,36}... | collective-permute-start | bytes 1572872 | tf_op jit(solution)/shard_map/ppermute | solution.py:10
  72.5 12.6 %collective-permute-start.5 = (f32[128,1024]{1,0:T(8,128)S(1)}, f32[128,1024]{1,0:T(8,128)S(1)}, u32[]{:S(2)}, u32[]{:S(2)}) collective-permute-start(f32[128,1024]{1,0:T(8,128)S(1)} %fusion.127), channel_id=1, source_target_pairs={{0,4},{4,8},{8,12},{12,16},{16,20},{20,24},{24,28},{28,32},{32,36}... | collective-permute-start | bytes 1572872 | tf_op jit(solution)/shard_map/ppermute | solution.py:10
  87.2 12.6 %collective-permute-start.6 = (f32[128,1024]{1,0:T(8,128)S(1)}, f32[128,1024]{1,0:T(8,128)S(1)}, u32[]{:S(2)}, u32[]{:S(2)}) collective-permute-start(f32[128,1024]{1,0:T(8,128)S(1)} %fusion.145), channel_id=1, source_target_pairs={{0,4},{4,8},{8,12},{12,16},{16,20},{20,24},{24,28},{28,32},{32,36}... | collective-permute-start | bytes 1572872 | tf_op jit(solution)/shard_map/ppermute | solution.py:10
  102.0 12.6 %collective-permute-start.7 = (f32[128,1024]{1,0:T(8,128)S(1)}, f32[128,1024]{1,0:T(8,128)S(1)}, u32[]{:S(2)}, u32[]{:S(2)}) collective-permute-start(f32[128,1024]{1,0:T(8,128)S(1)} %fusion.163), channel_id=1, source_target_pairs={{0,4},{4,8},{8,12},{12,16},{16,20},{20,24},{24,28},{28,32},{32,36}... | collective-permute-start | bytes 1572872 | tf_op jit(solution)/shard_map/ppermute | solution.py:10
  116.7 12.6 %collective-permute-start.8 = (f32[128,1024]{1,0:T(8,128)S(1)}, f32[128,1024]{1,0:T(8,128)S(1)}, u32[]{:S(2)}, u32[]{:S(2)}) collective-permute-start(f32[128,1024]{1,0:T(8,128)S(1)} %fusion.181), channel_id=1, source_target_pairs={{0,4},{4,8},{8,12},{12,16},{16,20},{20,24},{24,28},{28,32},{32,36}... | collective-permute-start | bytes 1572872 | tf_op jit(solution)/shard_map/ppermute | solution.py:10
  131.5 15.0 %collective-permute-start.10 = (f32[128,1024]{1,0:T(8,128)S(1)}, f32[128,1024]{1,0:T(8,128)S(1)}, u32[]{:S(2)}, u32[]{:S(2)}) collective-permute-start(f32[128,1024]{1,0:T(8,128)S(1)} %fusion.199), channel_id=1, source_target_pairs={{0,16},{4,20},{8,24},{12,28},{16,32},{20,36},{24,40},{28,44},{32,4... | collective-permute-start | bytes 1572872 | tf_op jit(solution)/shard_map/ppermute | solution.py:10
  133.4 23.3 %collective-permute-start.9 = (f32[128,1024]{1,0:T(8,128)S(1)}, f32[128,1024]{1,0:T(8,128)S(1)}, u32[]{:S(2)}, u32[]{:S(2)}) collective-permute-start(f32[128,1024]{1,0:T(8,128)S(1)} %fusion.199), channel_id=1, source_target_pairs={{0,4},{4,8},{8,12},{12,16},{16,20},{20,24},{24,28},{28,32},{32,36}... | collective-permute-start | bytes 1572872 | tf_op jit(solution)/shard_map/ppermute | solution.py:10
  158.9 15.1 %collective-permute-start = (f32[128,1024]{1,0:T(8,128)}, f32[128,1024]{1,0:T(8,128)S(1)}, u32[]{:S(2)}, u32[]{:S(2)}) collective-permute-start(f32[128,1024]{1,0:T(8,128)} %get-tuple-element.119), channel_id=1, source_target_pairs={{0,16},{4,20},{8,24},{12,28},{16,32},{20,36},{24,40},{28,44},{32,4... | collective-permute-start | bytes 1572872 | tf_op jit(solution)/shard_map/while/body/eval_jaxpr/ppermute | solution.py:10
  176.9 15.1 %collective-permute-start = (f32[128,1024]{1,0:T(8,128)}, f32[128,1024]{1,0:T(8,128)S(1)}, u32[]{:S(2)}, u32[]{:S(2)}) collective-permute-start(f32[128,1024]{1,0:T(8,128)} %get-tuple-element.119), channel_id=1, source_target_pairs={{0,16},{4,20},{8,24},{12,28},{16,32},{20,36},{24,40},{28,44},{32,4... | collective-permute-start | bytes 1572872 | tf_op jit(solution)/shard_map/while/body/eval_jaxpr/ppermute | solution.py:10
  194.9 15.3 %collective-permute-start = (f32[128,1024]{1,0:T(8,128)}, f32[128,1024]{1,0:T(8,128)S(1)}, u32[]{:S(2)}, u32[]{:S(2)}) collective-permute-start(f32[128,1024]{1,0:T(8,128)} %get-tuple-element.119), channel_id=1, source_target_pairs={{0,16},{4,20},{8,24},{12,28},{16,32},{20,36},{24,40},{28,44},{32,4... | collective-permute-start | bytes 1572872 | tf_op jit(solution)/shard_map/while/body/eval_jaxpr/ppermute | solution.py:10
  213.1 14.5 %collective-permute-start = (f32[128,1024]{1,0:T(8,128)}, f32[128,1024]{1,0:T(8,128)S(1)}, u32[]{:S(2)}, u32[]{:S(2)}) collective-permute-start(f32[128,1024]{1,0:T(8,128)} %get-tuple-element.119), channel_id=1, source_target_pairs={{0,16},{4,20},{8,24},{12,28},{16,32},{20,36},{24,40},{28,44},{32,4... | collective-permute-start | bytes 1572872 | tf_op jit(solution)/shard_map/while/body/eval_jaxpr/ppermute | solution.py:10
  230.4 13.7 %collective-permute-start = (f32[128,1024]{1,0:T(8,128)}, f32[128,1024]{1,0:T(8,128)S(1)}, u32[]{:S(2)}, u32[]{:S(2)}) collective-permute-start(f32[128,1024]{1,0:T(8,128)} %get-tuple-element.119), channel_id=1, source_target_pairs={{0,16},{4,20},{8,24},{12,28},{16,32},{20,36},{24,40},{28,44},{32,4... | collective-permute-start | bytes 1572872 | tf_op jit(solution)/shard_map/while/body/eval_jaxpr/ppermute | solution.py:10
  247.0 13.7 %collective-permute-start = (f32[128,1024]{1,0:T(8,128)}, f32[128,1024]{1,0:T(8,128)S(1)}, u32[]{:S(2)}, u32[]{:S(2)}) collective-permute-start(f32[128,1024]{1,0:T(8,128)} %get-tuple-element.119), channel_id=1, source_target_pairs={{0,16},{4,20},{8,24},{12,28},{16,32},{20,36},{24,40},{28,44},{32,4... | collective-permute-start | bytes 1572872 | tf_op jit(solution)/shard_map/while/body/eval_jaxpr/ppermute | solution.py:10
  263.6 13.7 %collective-permute-start = (f32[128,1024]{1,0:T(8,128)}, f32[128,1024]{1,0:T(8,128)S(1)}, u32[]{:S(2)}, u32[]{:S(2)}) collective-permute-start(f32[128,1024]{1,0:T(8,128)} %get-tuple-element.119), channel_id=1, source_target_pairs={{0,16},{4,20},{8,24},{12,28},{16,32},{20,36},{24,40},{28,44},{32,4... | collective-permute-start | bytes 1572872 | tf_op jit(solution)/shard_map/while/body/eval_jaxpr/ppermute | solution.py:10
  280.1 15.8 %collective-permute-start = (f32[128,1024]{1,0:T(8,128)}, f32[128,1024]{1,0:T(8,128)S(1)}, u32[]{:S(2)}, u32[]{:S(2)}) collective-permute-start(f32[128,1024]{1,0:T(8,128)} %get-tuple-element.119), channel_id=1, source_target_pairs={{0,16},{4,20},{8,24},{12,28},{16,32},{20,36},{24,40},{28,44},{32,4... | collective-permute-start | bytes 1572872 | tf_op jit(solution)/shard_map/while/body/eval_jaxpr/ppermute | solution.py:10
  298.9 44.4 %copy-start = (bf16[4,1024,1024]{2,1,0:T(8,128)(2,1)S(1)}, bf16[4,1024,1024]{2,1,0:T(8,128)(2,1)}, u32[]{:S(2)}) copy-start(bf16[4,1024,1024]{2,1,0:T(8,128)(2,1)} %get-tuple-element.134) | copy-start | bytes 25165828
  300.9 12.7 %collective-permute-start.11 = (f32[128,1024]{1,0:T(8,128)S(1)}, f32[128,1024]{1,0:T(8,128)S(1)}, u32[]{:S(2)}, u32[]{:S(2)}) collective-permute-start(f32[128,1024]{1,0:T(8,128)S(1)} %get-tuple-element.58), channel_id=1, source_target_pairs={{0,4},{4,8},{8,12},{12,16},{16,20},{20,24},{24,28},{28,32},{32,36}... | collective-permute-start | bytes 1572872 | tf_op jit(solution)/shard_map/ppermute | solution.py:10
  315.8 12.6 %collective-permute-start.12 = (f32[128,1024]{1,0:T(8,128)S(1)}, f32[128,1024]{1,0:T(8,128)S(1)}, u32[]{:S(2)}, u32[]{:S(2)}) collective-permute-start(f32[128,1024]{1,0:T(8,128)S(1)} %fusion.247), channel_id=1, source_target_pairs={{0,4},{4,8},{8,12},{12,16},{16,20},{20,24},{24,28},{28,32},{32,36}... | collective-permute-start | bytes 1572872 | tf_op jit(solution)/shard_map/ppermute | solution.py:10
  330.5 27.5 %copy-start.2 = (bf16[1,128,1024]{2,1,0:T(8,128)(2,1)S(1)}, bf16[1,128,1024]{2,1,0:T(8,128)(2,1)}, u32[]{:S(2)}) copy-start(bf16[1,128,1024]{2,1,0:T(8,128)(2,1)} %param.11) | copy-start | bytes 786436
  330.6 12.7 %collective-permute-start.13 = (f32[128,1024]{1,0:T(8,128)S(1)}, f32[128,1024]{1,0:T(8,128)S(1)}, u32[]{:S(2)}, u32[]{:S(2)}) collective-permute-start(f32[128,1024]{1,0:T(8,128)S(1)} %fusion.265), channel_id=1, source_target_pairs={{0,4},{4,8},{8,12},{12,16},{16,20},{20,24},{24,28},{28,32},{32,36}... | collective-permute-start | bytes 1572872 | tf_op jit(solution)/shard_map/ppermute | solution.py:10
  343.9 12.6 %collective-permute-start.14 = (f32[128,1024]{1,0:T(8,128)S(1)}, f32[128,1024]{1,0:T(8,128)S(1)}, u32[]{:S(2)}, u32[]{:S(2)}) collective-permute-start(f32[128,1024]{1,0:T(8,128)S(1)} %fusion.283), channel_id=1, source_target_pairs={{0,4},{4,8},{8,12},{12,16},{16,20},{20,24},{24,28},{28,32},{32,36}... | collective-permute-start | bytes 1572872 | tf_op jit(solution)/shard_map/ppermute | solution.py:10
  360.0 13.4 %all-to-all-start.1 = ((bf16[128,4,256]{2,0,1:T(8,128)(2,1)}), bf16[128,4,256]{2,0,1:T(8,128)(2,1)S(1)}, u32[]{:S(2)}, u32[]{:S(2)}) async-start(bf16[128,4,256]{2,0,1:T(8,128)(2,1)} %bitcast.312), calls=%async_computation.1 | async-start | bytes 524288 | tf_op jit(solution)/shard_map/all_to_all | solution.py:93
where the time goes:
time: 390 us; the launch traced here: 388 us
  waiting for transfers between devices  237 us (61%)
  matrix products  65.8 us (17%)
  starting transfers between devices  60.4 us (15%)
  blocking collectives  13.3 us (3%)
  local copies, waits for them, and re-layouts  8.5 us (2%)
    ppermute x22, waiting for transfers between devices, passed_along(): return lax.ppermute(shard, axis, pairs)  229 us
    dot_general x31, matrix products, advance(): jnp.dot(layer_state.astype(jnp.bfloat16), weight, preferred_element_type=...  64.4 us
    ppermute x22, starting transfers between devices, passed_along(): return lax.ppermute(shard, axis, pairs)  55.1 us
    all_to_all x1, blocking collectives, sent_to_all(): lax.all_to_all(jnp.broadcast_to(shard[None], (devices, *shard.shape)), ax...  13.3 us
    all_to_all x1, waiting for transfers between devices, body(): lax.all_to_all(deltas, 'dp', split_axis=1, concat_axis=0, tiled=True)  7.91 us
  transfers between devices with their start and end apart: 23, of which 23 were waited for; matrix products, arithmetic and copies ran while one was open for 3% of the time, Pallas kernels for 0%

commit v1 on v0

v1 whole, which is shorter than its diff:
```python
import functools

import jax
import jax.numpy as jnp
from jax import lax
from jax.experimental import pallas as pl
from jax.experimental.pallas import tpu as pltpu
from jax.sharding import PartitionSpec as P

MESH = pl.DeviceIdType.MESH
F32, BF16 = jnp.float32, jnp.bfloat16
CHUNK = 16
HALF = 64


def kernel(
    blocks,
    inputs,
    guesses,
    weights,
    biases,
    adjoint,
    new_out,
    coarse_out,
    grad_out,
    w_v,
    state,
    guess_in,
    relaxed,
    relaxed_in,
    forcing,
    first_v,
    update,
    level_in,
    below_in,
    below_step,
    solved,
    solved_in,
    final_v,
    final_in,
    early_send,
    early_in,
    a_all,
    d_send,
    d_all,
    w_sem,
    half_send,
    half_recv,
    level_send,
    level_recv,
    below_send,
    below_recv,
    solved_send,
    solved_recv,
    final_send,
    final_recv,
    early_sem,
    a_send,
    a_recv,
    d_ssem,
    d_rsem,
):
    rows = inputs.shape[0]
    chunks, halves = rows // CHUNK, rows // HALF
    h = 4.0 / (4 * blocks)
    me, zed = lax.axis_index("layer"), lax.axis_index("dp")
    planes = a_all.shape[0]
    pos = lax.rem(me + 1, 4)
    is_first, is_last = me == 0, me == blocks - 1
    is_c = pos == 0

    for layer in range(4):
        pltpu.make_async_copy(weights.at[layer], w_v.at[layer], w_sem.at[layer]).start()

    right, left = lax.rem(zed + 1, planes), lax.rem(zed + planes - 1, planes)
    across = lax.rem(zed + 2, planes)
    barrier = pltpu.get_barrier_semaphore()
    for step in (1, blocks - 1, 4, blocks - 4):
        pl.semaphore_signal(
            barrier, inc=1, device_id=(lax.rem(me + step, blocks), zed), device_id_type=MESH
        )
    for other in (right, left, across):
        pl.semaphore_signal(barrier, inc=1, device_id=(me, other), device_id_type=MESH)
    pl.semaphore_wait(barrier, 7)

    def hop(src, dst, send_sem, recv_sem, by):
        return pltpu.make_async_remote_copy(
            src_ref=src,
            dst_ref=dst,
            send_sem=send_sem,
            recv_sem=recv_sem,
            device_id=(lax.rem(me + by, blocks), zed),
            device_id_type=MESH,
        )

    def zhop(src, dst, send_sem, recv_sem, to):
        return pltpu.make_async_remote_copy(
            src_ref=src,
            dst_ref=dst,
            send_sem=send_sem,
            recv_sem=recv_sem,
            device_id=(me, to),
            device_id_type=MESH,
        )

    def chunk_rows(c):
        return pl.ds(pl.multiple_of(c * CHUNK, CHUNK), CHUNK)

    def half_rows(c):
        return pl.ds(pl.multiple_of(c * HALF, HALF), HALF)

    def act(x, layer):
        z = jnp.dot(x.astype(BF16), w_v[layer], preferred_element_type=F32) + biases[layer]
        return jnp.tanh(z)

    def each(count, body):
        def step(c, carry):
            body(c)
            return carry

        lax.fori_loop(0, count, step, 0)

    def guess_hop(c):
        r = half_rows(c)
        return hop(guesses.at[0, r], guess_in.at[r], half_send.at[0, c], half_recv.at[0, c], 1)

    @pl.when(jnp.logical_not(is_last))
    def _():
        each(halves, lambda c: guess_hop(c).start())

    @pl.when(is_first)
    def _():
        guess_in[...] = inputs[...]
        relaxed_in[...] = inputs[...]

    for layer in range(4):
        pltpu.make_async_copy(weights.at[layer], w_v.at[layer], w_sem.at[layer]).wait()

    def relaxed_hop(c):
        r = half_rows(c)
        return hop(relaxed.at[r], relaxed_in.at[r], half_send.at[1, c], half_recv.at[1, c], 1)

    def relax_half(c):
        r = half_rows(c)

        @pl.when(jnp.logical_not(is_first))
        def _():
            guess_hop(c).wait_recv()

        relaxed[r, :] = guess_in[r, :]

        def layer_step(layer, carry):
            u = relaxed[r, :]
            relaxed[r, :] = u + h * act(u, layer)
            return carry

        lax.fori_loop(0, 4, layer_step, 0)

        @pl.when(jnp.logical_not(is_last))
        def _():
            relaxed_hop(c).start()

    each(halves, relax_half)

    def forcing_half(c):
        r = half_rows(c)

        @pl.when(jnp.logical_not(is_first))
        def _():
            relaxed_hop(c).wait_recv()

        u = relaxed_in[r, :]
        t = act(u, 0)
        coarse = u + (4.0 * h) * t
        first_v[r, :] = coarse
        state[r, :] = u + h * t

        def layer_step(layer, carry):
            u = state[r, :]
            state[r, :] = u + h * act(u, layer)
            return carry

        lax.fori_loop(1, 4, layer_step, 0)
        force = state[r, :] - first_v[r, :]
        forcing[r, :] = force
        first_v[r, :] = first_v[r, :] + force

    each(halves, forcing_half)

    slot = jnp.where(is_c, 1, 0)

    def level_hop(sweep, c, src):
        r = chunk_rows(c)
        return hop(
            src.at[r], level_in.at[sweep, r], level_send.at[sweep, c], level_recv.at[sweep, c], 1
        )

    def first_hop(c):
        r = chunk_rows(c)
        return hop(
            first_v.at[r], level_in.at[slot, r], level_send.at[0, c], level_recv.at[slot, c], 1
        )

    def below_hop(c):
        r = chunk_rows(c)
        return hop(first_v.at[r], below_in.at[r], below_send.at[c], below_recv.at[c], 4)

    def first_sweep(c):
        r = chunk_rows(c)

        @pl.when(pos != 1)
        def _():
            level_hop(0, c, first_v).wait_recv()
            u = level_in[0, r, :]
            first_v[r, :] = u + (4.0 * h) * act(u, 0) + forcing[r, :]

        @pl.when(jnp.logical_not(is_last))
        def _():
            first_hop(c).start()

        @pl.when(jnp.logical_and(is_c, jnp.logical_not(is_last)))
        def _():
            below_hop(c).start()

    each(chunks, first_sweep)

    @pl.when(is_c)
    def _():
        def below_chunk(c):
            r = chunk_rows(c)

            @pl.when(me >= 4)
            def _():
                below_hop(c).wait_recv()

            @pl.when(me < 4)
            def _():
                below_in[r, :] = inputs[r, :]

            u = below_in[r, :]
            below_step[r, :] = u + (16.0 * h) * act(u, 0)

        each(chunks, below_chunk)

    @pl.when(is_first)
    def _():
        level_in[1] = inputs[...]

    def second_sweep(c):
        r = chunk_rows(c)

        @pl.when(jnp.logical_not(is_first))
        def _():
            level_hop(1, c, update).wait_recv()

        u = level_in[1, r, :]
        update[r, :] = u + (4.0 * h) * act(u, 0) + forcing[r, :]

        @pl.when(jnp.logical_not(is_c))
        def _():
            level_hop(1, c, update).start()

    each(chunks, second_sweep)

    def early_hop():
        return hop(early_send, early_in, early_sem.at[0], early_sem.at[1], 4)

    @pl.when(jnp.logical_not(is_c))
    def _():
        early_send[...] = update[...].astype(BF16)

        @pl.when(me < blocks - 4)
        def _():
            early_hop().start()

        @pl.when(me >= 4)
        def _():
            early_hop().wait_recv()

        @pl.when(me < 4)
        def _():
            early_in[...] = inputs[...].astype(BF16)

        below_step[...] = early_in[...].astype(F32) + (16.0 * h) * act(early_in[...], 0)
        step_two = below_step[...]
        coarse_out[0] = step_two + (update[...] - step_two) - relaxed[...]

    def solved_hop(c):
        r = chunk_rows(c)
        return hop(solved.at[r], solved_in.at[r], solved_send.at[c], solved_recv.at[c], 4)

    def final_hop(c, src):
        r = chunk_rows(c)
        return hop(src.at[r], final_in.at[r], final_send.at[c], final_recv.at[c], 1)

    @pl.when(is_c)
    def _():
        def solve_chunk(c):
            r = chunk_rows(c)
            force = update[r, :] - below_step[r, :]

            @pl.when(me >= 4)
            def _():
                solved_hop(c).wait_recv()
                u = solved_in[r, :]
                solved[r, :] = u + (16.0 * h) * act(u, 0) + force

            @pl.when(me < 4)
            def _():
                solved[r, :] = below_step[r, :] + force

            @pl.when(jnp.logical_not(is_last))
            def _():
                solved_hop(c).start()
                final_hop(c, solved).start()

            coarse_out[0, r, :] = solved[r, :] - relaxed[r, :]

        each(chunks, solve_chunk)

    @pl.when(is_first)
    def _():
        final_in[...] = inputs[...]

    def final_sweep(c):
        r = chunk_rows(c)

        @pl.when(jnp.logical_not(is_first))
        def _():
            final_hop(c, final_v).wait_recv()

        u = final_in[r, :]
        t = act(u, 0)
        final_v[r, :] = u + (4.0 * h) * t + forcing[r, :]

        @pl.when(jnp.logical_not(is_c))
        def _():
            final_hop(c, final_v).start()

        state[r, :] = u + h * t

    each(chunks, final_sweep)

    def a_hop(side, c):
        r = half_rows(c)
        return zhop(
            a_all.at[zed, r],
            a_all.at[zed, r],
            a_send.at[side, c],
            a_recv.at[side, c],
            right if side == 0 else left,
        )

    def a_came(side, c):
        r = half_rows(c)
        source = left if side == 0 else right
        return zhop(
            a_all.at[source, r],
            a_all.at[source, r],
            a_send.at[side, c],
            a_recv.at[side, c],
            right if side == 0 else left,
        )

    def a_relay(side):
        r = half_rows(side)
        source = left if side == 0 else right
        return zhop(
            a_all.at[source, r],
            a_all.at[source, r],
            a_send.at[2, side],
            a_recv.at[2, side],
            right if side == 0 else left,
        )

    def a_relayed(side):
        r = half_rows(side)
        return zhop(
            a_all.at[across, r],
            a_all.at[across, r],
            a_send.at[2, side],
            a_recv.at[2, side],
            right if side == 0 else left,
        )

    def d_hop(j, c):
        r = half_rows(c)
        to = lax.rem(zed + j, planes)
        return zhop(
            d_send.at[to, r], d_all.at[zed, r], d_ssem.at[j - 1, c], d_rsem.at[j - 1, c], to
        )

    def d_came(j, c):
        r = half_rows(c)
        source = lax.rem(zed + planes - j, planes)
        return zhop(
            d_send.at[zed, r], d_all.at[source, r], d_ssem.at[j - 1, c], d_rsem.at[j - 1, c], source
        )

    cols = grad_out.shape[2]

    def block_half(c):
        r = half_rows(c)

        def layer_step(layer, carry):
            u = state[r, :]
            state[r, :] = u + h * act(u, layer)
            return carry

        lax.fori_loop(1, 3, layer_step, 0)
        u = state[r, :]
        x = u.astype(BF16)
        a_all[zed, r, :] = x
        a_hop(0, c).start()
        a_hop(1, c).start()
        t = act(x, 3)
        new_out[0, r, :] = u + h * t
        delta = (adjoint[0, r, :].astype(F32) * h * (1.0 - t * t)).astype(BF16)
        for j in range(planes):
            d_send[j, r, :] = delta[:, j * cols : (j + 1) * cols]
        d_all[zed, r, :] = d_send[zed, r, :]
        for j in range(1, planes):
            d_hop(j, c).start()

    each(halves, block_half)

    for side in range(2):
        a_came(side, side).wait_recv()
        a_relay(side).start()
    for side in range(2):
        a_came(side, 1 - side).wait_recv()
    for j in range(1, planes):
        for c in range(halves):
            d_came(j, c).wait_recv()
    for side in range(2):
        a_relayed(side).wait_recv()
    grad_out[0] = lax.dot_general(
        a_all[...].reshape(planes * rows, a_all.shape[2]),
        d_all[...].reshape(planes * rows, cols),
        (((0,), (0,)), ((), ())),
        preferred_element_type=F32,
    )

    @pl.when(jnp.logical_not(is_last))
    def _():
        def sent(c):
            guess_hop(c).wait_send()
            relaxed_hop(c).wait_send()

        each(halves, sent)

        def sent_chunk(c):
            first_hop(c).wait_send()
            final_hop(c, final_v).wait_send()

        each(chunks, sent_chunk)

    @pl.when(jnp.logical_not(is_c))
    def _():
        each(chunks, lambda c: level_hop(1, c, update).wait_send())

        @pl.when(me < blocks - 4)
        def _():
            early_hop().wait_send()

    @pl.when(jnp.logical_and(is_c, jnp.logical_not(is_last)))
    def _():
        def sent_c(c):
            below_hop(c).wait_send()
            solved_hop(c).wait_send()

        each(chunks, sent_c)

    for side in range(2):
        for c in range(halves):
            a_hop(side, c).wait_send()
        a_relay(side).wait_send()
    for j in range(1, planes):
        for c in range(halves):
            d_hop(j, c).wait_send()


def solution(mesh):
    blocks, planes = mesh.shape["layer"], mesh.shape["dp"]

    def body(inputs, guesses, weights, biases, adjoint):
        rows, width = inputs.shape
        cols = width // planes
        chunks, halves = rows // CHUNK, rows // HALF
        whole = pltpu.VMEM((rows, width), F32)
        dma = pltpu.SemaphoreType.DMA
        vmem = pl.BlockSpec(memory_space=pltpu.VMEM)
        return pl.pallas_call(
            functools.partial(kernel, blocks),
            out_shape=(
                jax.ShapeDtypeStruct((1, rows, width), F32),
                jax.ShapeDtypeStruct((1, rows, width), F32),
                jax.ShapeDtypeStruct((1, width, cols), F32),
            ),
            in_specs=[vmem, vmem, pl.BlockSpec(memory_space=pl.ANY), vmem, vmem],
            out_specs=(vmem, vmem, vmem),
            scratch_shapes=[
                pltpu.VMEM((4, width, width), BF16),
                whole,
                whole,
                whole,
                whole,
                whole,
                whole,
                whole,
                pltpu.VMEM((2, rows, width), F32),
                whole,
                whole,
                whole,
                whole,
                whole,
                whole,
                pltpu.VMEM((rows, width), BF16),
                pltpu.VMEM((rows, width), BF16),
                pltpu.VMEM((planes, rows, width), BF16),
                pltpu.VMEM((planes, rows, cols), BF16),
                pltpu.VMEM((planes, rows, cols), BF16),
                dma((4,)),
                dma((2, halves)),
                dma((2, halves)),
                dma((2, chunks)),
                dma((2, chunks)),
                dma((chunks,)),
                dma((chunks,)),
                dma((chunks,)),
                dma((chunks,)),
                dma((chunks,)),
                dma((chunks,)),
                dma((2,)),
                dma((3, halves)),
                dma((3, halves)),
                dma((planes - 1, halves)),
                dma((planes - 1, halves)),
            ],
            compiler_params=pltpu.CompilerParams(
                collective_id=0, has_side_effects=True, vmem_limit_bytes=60 * 1024 * 1024
            ),
            name="mgrit_cycle",
        )(inputs, guesses, weights, biases.reshape(4, 1, width), adjoint)

    return jax.shard_map(
        body,
        mesh=mesh,
        in_specs=(
            P("dp", None),
            P("layer", "dp", None),
            P("layer", None, None),
            P("layer", None),
            P("layer", "dp", None),
        ),
        out_specs=(P("layer", "dp", None), P("layer", "dp", None), P("layer", None, "dp")),
        check_vma=False,
    )
```

time: 390 us -> 100 us (0.26)
  the two profiles are of different devices: /device:TPU:16 before, /device:TPU:31 now
where the time goes in v1:
time: 100 us
  Pallas kernels  92.1 us (92%)
  local copies, waits for them, and re-layouts  7.36 us (7%)
    pallas_call x1, Pallas kernels, body(): pl.pallas_call(functools.partial(kernel, blocks), out_shape=(jax.ShapeDty...  92.1 us
    unnamed x3, local copies, waits for them, and re-layouts  6.03 us

profile of v1, /device:TPU:31, one launch (start us, length us, event | category | flops | bytes accessed | tf_op | source)
XLA Modules:
  0.0 100.1 jit_solution(8065645151093804437)
XLA Ops:
  0.6 1.3 %reshape.9.biases = f32[4,1,1024]{2,1,0:T(1,128)} reshape(f32[4,1024]{1,0:T(4,128)} %param.8) | data formatting | bytes 32768 | tf_op jit(solution)/shard_map/reshape | solution.py:544
  2.0 92.1 %mgrit_cycle.1 = (f32[1,128,1024]{2,1,0:T(8,128)}, f32[1,128,1024]{2,1,0:T(8,128)}, f32[1,1024,256]{2,1,0:T(8,128)}) custom-call(f32[128,1024]{1,0:T(8,128)} %inputs.1, f32[1,128,1024]{2,1,0:T(8,128)} %guesses.1, bf16[4,1024,1024]{2,1,0:T(8,128)(2,1)} %weights.1, f32[4,1,1024]{2,1,0:T(1,128)} %reshape.9.biases, bf16[1,128,1024]{2,1,0:T(8,128)(2,1)} %adjoint.1), custom_call_target="tpu_custom_call" | custom-call | tf_op jit(solution)/shard_map/mgrit_cycle/pallas_call | solution.py:493
  94.0 1.9 %copy.11 = f32[1,128,1024]{2,1,0:T(8,128)} copy(f32[1,128,1024]{2,1,0:T(8,128)} %get-tuple-element.6) | data formatting | bytes 1048576
  95.9 1.9 %copy.12 = f32[1,128,1024]{2,1,0:T(8,128)} copy(f32[1,128,1024]{2,1,0:T(8,128)} %get-tuple-element.7) | data formatting | bytes 1048576
  97.8 2.3 %copy.13 = f32[1,1024,256]{2,1,0:T(8,128)} copy(f32[1,1024,256]{2,1,0:T(8,128)} %get-tuple-element.8) | data formatting | bytes 2097152

commit v2 on v1

--- a/solution.py
+++ b/solution.py
@@ -11,6 +11,7 @@
 F32, BF16 = jnp.float32, jnp.bfloat16
 CHUNK = 16
 HALF = 64
+PIECES = 8
 
 
 def kernel(
@@ -34,10 +35,21 @@
     level_in,
     below_in,
     below_step,
+    own_step,
     solved,
+    solved_a,
     solved_in,
+    solved_back,
     final_v,
     final_in,
+    v_mid,
+    v_in,
+    u_mid,
+    u_in,
+    w_mid,
+    w_pair,
+    b_send,
+    b_pair,
     early_send,
     early_in,
     a_all,
@@ -54,6 +66,17 @@
     solved_recv,
     final_send,
     final_recv,
+    back_send,
+    back_recv,
+    mid_send,
+    mid_recv,
+    far_send,
+    far_recv,
+    wmid_send,
+    wmid_recv,
+    wfar_send,
+    wfar_recv,
+    b_sem,
     early_sem,
     a_send,
     a_recv,
@@ -68,6 +91,9 @@
     pos = lax.rem(me + 1, 4)
     is_first, is_last = me == 0, me == blocks - 1
     is_c = pos == 0
+    seat, row = lax.rem(me, 8), me // 8
+    is_a, is_pair, is_relay = seat == 3, seat == 7, seat == 1
+    last_row = blocks // 8 - 1
 
     for layer in range(4):
         pltpu.make_async_copy(weights.at[layer], w_v.at[layer], w_sem.at[layer]).start()
@@ -75,13 +101,14 @@
     right, left = lax.rem(zed + 1, planes), lax.rem(zed + planes - 1, planes)
     across = lax.rem(zed + 2, planes)
     barrier = pltpu.get_barrier_semaphore()
-    for step in (1, blocks - 1, 4, blocks - 4):
+    near = (1, 2, 3, 4, 6, 8)
+    for step in near + tuple(blocks - step for step in near):
         pl.semaphore_signal(
             barrier, inc=1, device_id=(lax.rem(me + step, blocks), zed), device_id_type=MESH
         )
     for other in (right, left, across):
         pl.semaphore_signal(barrier, inc=1, device_id=(me, other), device_id_type=MESH)
-    pl.semaphore_wait(barrier, 7)
+    pl.semaphore_wait(barrier, 2 * len(near) + 3)
 
     def hop(src, dst, send_sem, recv_sem, by):
         return pltpu.make_async_remote_copy(
@@ -89,7 +116,7 @@
             dst_ref=dst,
             send_sem=send_sem,
             recv_sem=recv_sem,
-            device_id=(lax.rem(me + by, blocks), zed),
+            device_id=(lax.rem(me + by + blocks, blocks), zed),
             device_id_type=MESH,
         )
 
@@ -110,8 +137,12 @@
         return pl.ds(pl.multiple_of(c * HALF, HALF), HALF)
 
     def act(x, layer):
-        z = jnp.dot(x.astype(BF16), w_v[layer], preferred_element_type=F32) + biases[layer]
-        return jnp.tanh(z)
+        z = jnp.dot(x.astype(BF16), w_v[layer], preferred_element_type=F32)
+        return jnp.tanh(z + biases[pl.ds(layer, 1), :])
+
+    def act_pair(x):
+        z = jnp.dot(x.astype(BF16), w_pair[...], preferred_element_type=F32)
+        return jnp.tanh(z + b_pair[0:1, :])
 
     def each(count, body):
         def step(c, carry):
@@ -133,8 +164,35 @@
         guess_in[...] = inputs[...]
         relaxed_in[...] = inputs[...]
 
-    for layer in range(4):
-        pltpu.make_async_copy(weights.at[layer], w_v.at[layer], w_sem.at[layer]).wait()
+    def piece_rows(i):
+        depth = weights.shape[1] // PIECES
+        return pl.ds(pl.multiple_of(i * depth, depth), depth)
+
+    def weight_mid(i):
+        r = piece_rows(i)
+        return hop(weights.at[0, r], w_mid.at[r], wmid_send.at[i], wmid_recv.at[i], -2)
+
+    def weight_far(i):
+        r = piece_rows(i)
+        return hop(w_mid.at[r], w_pair.at[r], wfar_send.at[i], wfar_recv.at[i], 6)
+
+    def bias_hop():
+        return hop(b_send, b_pair, b_sem.at[0], b_sem.at[1], 4)
+
+    @pl.when(is_a)
+    def _():
+        each(PIECES, lambda i: weight_mid(i).start())
+        b_send[...] = jnp.broadcast_to(biases[0:1, :], b_send.shape)
+        bias_hop().start()
+
+    def relay_weights(start, stop):
+        @pl.when(is_relay)
+        def _():
+            def forward(i):
+                weight_mid(start + i).wait_recv()
+                weight_far(start + i).start()
+
+            each(stop - start, forward)
 
     def relaxed_hop(c):
         r = half_rows(c)
@@ -150,6 +208,10 @@
         relaxed[r, :] = guess_in[r, :]
 
         def layer_step(layer, carry):
+            @pl.when(c == 0)
+            def _():
+                pltpu.make_async_copy(weights.at[layer], w_v.at[layer], w_sem.at[layer]).wait()
+
             u = relaxed[r, :]
             relaxed[r, :] = u + h * act(u, layer)
             return carry
@@ -161,6 +223,7 @@
             relaxed_hop(c).start()
 
     each(halves, relax_half)
+    relay_weights(0, 2)
 
     def forcing_half(c):
         r = half_rows(c)
@@ -186,6 +249,7 @@
         first_v[r, :] = first_v[r, :] + force
 
     each(halves, forcing_half)
+    relay_weights(2, 5)
 
     slot = jnp.where(is_c, 1, 0)
 
@@ -203,7 +267,19 @@
 
     def below_hop(c):
         r = chunk_rows(c)
-        return hop(first_v.at[r], below_in.at[r], below_send.at[c], below_recv.at[c], 4)
+        return hop(first_v.at[r], below_in.at[r], below_send.at[c], below_recv.at[c], 8)
+
+    def mid_hop(kind, c, src):
+        r = chunk_rows(c)
+        dst = (v_mid, u_mid)[kind]
+        return hop(src.at[r], dst.at[r], mid_send.at[kind, c], mid_recv.at[kind, c], -2)
+
+    def far_hop(kind, c):
+        r = chunk_rows(c)
+        src, dst = ((v_mid, v_in), (u_mid, u_in))[kind]
+        return hop(src.at[r], dst.at[r], far_send.at[kind, c], far_recv.at[kind, c], 6)
+
+    pair_goes_on = jnp.logical_and(is_pair, row < last_row)
 
     def first_sweep(c):
         r = chunk_rows(c)
@@ -218,105 +294,132 @@
         def _():
             first_hop(c).start()
 
-        @pl.when(jnp.logical_and(is_c, jnp.logical_not(is_last)))
+        @pl.when(is_a)
+        def _():
+            mid_hop(0, c, first_v).start()
+
+        @pl.when(pair_goes_on)
         def _():
             below_hop(c).start()
 
     each(chunks, first_sweep)
-
-    @pl.when(is_c)
-    def _():
-        def below_chunk(c):
+    relay_weights(5, PIECES)
+
+    @pl.when(is_pair)
+    def _():
+        each(chunks, lambda c: far_hop(0, c).wait_recv())
+        u = v_in[...]
+        own_step[...] = u + (16.0 * h) * act(u, 0)
+
+    is_fourth = me == 3
+
+    @pl.when(is_fourth)
+    def _():
+        u = inputs[...]
+        below_step[...] = u + (16.0 * h) * act(u, 0)
+
+    @pl.when(is_first)
+    def _():
+        level_in[1] = inputs[...]
+
+    def solved_hop(c):
+        r = chunk_rows(c)
+        return hop(solved.at[r], solved_in.at[r], solved_send.at[c], solved_recv.at[c], 8)
+
+    def back_hop(c):
+        r = chunk_rows(c)
+        return hop(solved_a.at[r], solved_back.at[r], back_send.at[0, c], back_recv.at[c], -4)
+
+    def final_hop(c, src):
+        r = chunk_rows(c)
+        return hop(src.at[r], final_in.at[r], final_send.at[c], final_recv.at[c], 1)
+
+    def final_a_hop(c):
+        r = chunk_rows(c)
+        return hop(solved_a.at[r], final_in.at[r], back_send.at[1, c], final_recv.at[c], -3)
+
+    def solve_chunk(c, w_a):
+        r = chunk_rows(c)
+        solved_a[r, :] = w_a
+        back_hop(c).start()
+        final_a_hop(c).start()
+        force = update[r, :] - own_step[r, :]
+        w_b = w_a + (16.0 * h) * act(w_a, 0) + force
+        solved[r, :] = w_b
+
+        @pl.when(row < last_row)
+        def _():
+            solved_hop(c).start()
+            final_hop(c, solved).start()
+
+        coarse_out[0, r, :] = w_b - relaxed[r, :]
+
+    pair_first = jnp.logical_and(is_pair, row == 0)
+
+    def second_sweep(c):
+        r = chunk_rows(c)
+
+        @pl.when(jnp.logical_not(is_first))
+        def _():
+            level_hop(1, c, update).wait_recv()
+
+        u = level_in[1, r, :]
+        new = u + (4.0 * h) * act(u, 0) + forcing[r, :]
+        update[r, :] = new
+
+        @pl.when(jnp.logical_not(is_c))
+        def _():
+            level_hop(1, c, update).start()
+
+        @pl.when(is_relay)
+        def _():
+            mid_hop(0, c, first_v).wait_recv()
+            far_hop(0, c).start()
+
+        @pl.when(is_fourth)
+        def _():
+            step_two = below_step[r, :]
+            update[r, :] = step_two + (new - step_two)
+
+        @pl.when(is_a)
+        def _():
+            mid_hop(1, c, update).start()
+
+        @pl.when(pair_first)
+        def _():
+            far_hop(1, c).wait_recv()
+            solve_chunk(c, u_in[r, :])
+
+    each(chunks, second_sweep)
+
+    @pl.when(is_relay)
+    def _():
+        def forward(c):
+            mid_hop(1, c, update).wait_recv()
+            far_hop(1, c).start()
+
+        each(chunks, forward)
+
+    @pl.when(is_pair)
+    def _():
+        each(PIECES, lambda i: weight_far(i).wait_recv())
+        bias_hop().wait_recv()
+
+    @pl.when(jnp.logical_and(is_pair, row > 0))
+    def _():
+        each(chunks, lambda c: below_hop(c).wait_recv())
+        u = below_in[...]
+        below_step[...] = u + (16.0 * h) * act_pair(u)
+
+        def solve_both(c):
             r = chunk_rows(c)
-
-            @pl.when(me >= 4)
-            def _():
-                below_hop(c).wait_recv()
-
-            @pl.when(me < 4)
-            def _():
-                below_in[r, :] = inputs[r, :]
-
-            u = below_in[r, :]
-            below_step[r, :] = u + (16.0 * h) * act(u, 0)
-
-        each(chunks, below_chunk)
-
-    @pl.when(is_first)
-    def _():
-        level_in[1] = inputs[...]
-
-    def second_sweep(c):
-        r = chunk_rows(c)
-
-        @pl.when(jnp.logical_not(is_first))
-        def _():
-            level_hop(1, c, update).wait_recv()
-
-        u = level_in[1, r, :]
-        update[r, :] = u + (4.0 * h) * act(u, 0) + forcing[r, :]
-
-        @pl.when(jnp.logical_not(is_c))
-        def _():
-            level_hop(1, c, update).start()
-
-    each(chunks, second_sweep)
-
-    def early_hop():
-        return hop(early_send, early_in, early_sem.at[0], early_sem.at[1], 4)
-
-    @pl.when(jnp.logical_not(is_c))
-    def _():
-        early_send[...] = update[...].astype(BF16)
-
-        @pl.when(me < blocks - 4)
-        def _():
-            early_hop().start()
-
-        @pl.when(me >= 4)
-        def _():
-            early_hop().wait_recv()
-
-        @pl.when(me < 4)
-        def _():
-            early_in[...] = inputs[...].astype(BF16)
-
-        below_step[...] = early_in[...].astype(F32) + (16.0 * h) * act(early_in[...], 0)
-        step_two = below_step[...]
-        coarse_out[0] = step_two + (update[...] - step_two) - relaxed[...]
-
-    def solved_hop(c):
-        r = chunk_rows(c)
-        return hop(solved.at[r], solved_in.at[r], solved_send.at[c], solved_recv.at[c], 4)
-
-    def final_hop(c, src):
-        r = chunk_rows(c)
-        return hop(src.at[r], final_in.at[r], final_send.at[c], final_recv.at[c], 1)
-
-    @pl.when(is_c)
-    def _():
-        def solve_chunk(c):
-            r = chunk_rows(c)
-            force = update[r, :] - below_step[r, :]
-
-            @pl.when(me >= 4)
-            def _():
-                solved_hop(c).wait_recv()
-                u = solved_in[r, :]
-                solved[r, :] = u + (16.0 * h) * act(u, 0) + force
-
-            @pl.when(me < 4)
-            def _():
-                solved[r, :] = below_step[r, :] + force
-
-            @pl.when(jnp.logical_not(is_last))
-            def _():
-                solved_hop(c).start()
-                final_hop(c, solved).start()
-
-            coarse_out[0, r, :] = solved[r, :] - relaxed[r, :]
-
-        each(chunks, solve_chunk)
+            far_hop(1, c).wait_recv()
+            force = u_in[r, :] - below_step[r, :]
+            solved_hop(c).wait_recv()
+            u = solved_in[r, :]
+            solve_chunk(c, u + (16.0 * h) * act_pair(u) + force)
+
+        each(chunks, solve_both)
 
     @pl.when(is_first)
     def _():
@@ -340,6 +443,16 @@
         state[r, :] = u + h * t
 
     each(chunks, final_sweep)
+
+    def early_hop():
+        return hop(early_send, early_in, early_sem.at[0], early_sem.at[1], 4)
+
+    sends_early = jnp.logical_and(jnp.logical_not(is_c), me < blocks - 4)
+
+    @pl.when(sends_early)
+    def _():
+        early_send[...] = update[...].astype(BF16)
+        early_hop().start()
 
     def a_hop(side, c):
         r = half_rows(c)
@@ -427,6 +540,26 @@
     for side in range(2):
         a_came(side, side).wait_recv()
         a_relay(side).start()
+
+    @pl.when(jnp.logical_not(is_c))
+    def _():
+        @pl.when(me >= 4)
+        def _():
+            early_hop().wait_recv()
+
+        @pl.when(me < 4)
+        def _():
+            early_in[...] = inputs[...].astype(BF16)
+
+        below_step[...] = early_in[...].astype(F32) + (16.0 * h) * act(early_in[...], 0)
+        step_two = below_step[...]
+        coarse_out[0] = step_two + (update[...] - step_two) - relaxed[...]
+
+    @pl.when(is_a)
+    def _():
+        each(chunks, lambda c: back_hop(c).wait_recv())
+        coarse_out[0] = solved_back[...] - relaxed[...]
+
     for side in range(2):
         a_came(side, 1 - side).wait_recv()
     for j in range(1, planes):
@@ -449,27 +582,57 @@
 
         each(halves, sent)
 
-        def sent_chunk(c):
-            first_hop(c).wait_send()
+        each(chunks, lambda c: first_hop(c).wait_send())
+
+    @pl.when(jnp.logical_not(is_c))
+    def _():
+        def sent(c):
+            level_hop(1, c, update).wait_send()
             final_hop(c, final_v).wait_send()
 
-        each(chunks, sent_chunk)
-
-    @pl.when(jnp.logical_not(is_c))
-    def _():
-        each(chunks, lambda c: level_hop(1, c, update).wait_send())
-
-        @pl.when(me < blocks - 4)
-        def _():
-            early_hop().wait_send()
-
-    @pl.when(jnp.logical_and(is_c, jnp.logical_not(is_last)))
-    def _():
-        def sent_c(c):
+        each(chunks, sent)
+
+    @pl.when(sends_early)
+    def _():
+        early_hop().wait_send()
+
+    @pl.when(is_a)
+    def _():
+        each(PIECES, lambda i: weight_mid(i).wait_send())
+        bias_hop().wait_send()
+
+        def sent(c):
+            mid_hop(0, c, first_v).wait_send()
+            mid_hop(1, c, update).wait_send()
+
+        each(chunks, sent)
+
+    @pl.when(is_relay)
+    def _():
+        each(PIECES, lambda i: weight_far(i).wait_send())
+
+        def sent(c):
+            far_hop(0, c).wait_send()
+            far_hop(1, c).wait_send()
+
+        each(chunks, sent)
+
+    @pl.when(is_pair)
+    def _():
+        def sent(c):
+            back_hop(c).wait_send()
+            final_a_hop(c).wait_send()
+
+        each(chunks, sent)
+
+    @pl.when(pair_goes_on)
+    def _():
+        def sent(c):
             below_hop(c).wait_send()
             solved_hop(c).wait_send()
-
-        each(chunks, sent_c)
+            final_hop(c, solved).wait_send()
+
+        each(chunks, sent)
 
     for side in range(2):
         for c in range(halves):
@@ -515,6 +678,17 @@
                 whole,
                 whole,
                 whole,
+                whole,
+                whole,
+                whole,
+                whole,
+                whole,
+                whole,
+                whole,
+                pltpu.VMEM((width, width), BF16),
+                pltpu.VMEM((width, width), BF16),
+                pltpu.VMEM((8, width), F32),
+                pltpu.VMEM((8, width), F32),
                 pltpu.VMEM((rows, width), BF16),
                 pltpu.VMEM((rows, width), BF16),
                 pltpu.VMEM((planes, rows, width), BF16),
@@ -531,6 +705,17 @@
                 dma((chunks,)),
                 dma((chunks,)),
                 dma((chunks,)),
+                dma((2, chunks)),
+                dma((chunks,)),
+                dma((2, chunks)),
+                dma((2, chunks)),
+                dma((2, chunks)),
+                dma((2, chunks)),
+                dma((PIECES,)),
+                dma((PIECES,)),
+                dma((PIECES,)),
+                dma((PIECES,)),
+                dma((2,)),
                 dma((2,)),
                 dma((3, halves)),
                 dma((3, halves)),
@@ -541,7 +726,7 @@
                 collective_id=0, has_side_effects=True, vmem_limit_bytes=60 * 1024 * 1024
             ),
             name="mgrit_cycle",
-        )(inputs, guesses, weights, biases.reshape(4, 1, width), adjoint)
+        )(inputs, guesses, weights, biases, adjoint)
 
     return jax.shard_map(
         body,

time: 100 us -> 99.9 us (level)
  local copies, waits for them, and re-layouts: 7.36 us -> 6.03 us
    reshape x1 -> x0, local copies, waits for them, and re-layouts: 1.33 us -> none  [body(): biases.reshape(4, 1, width)]
where the time goes in v2:
time: 99.9 us; the launch traced here: 99.6 us
  Pallas kernels  93 us (93%)
  local copies, waits for them, and re-layouts  6.03 us (6%)
    pallas_call x1, Pallas kernels, body(): pl.pallas_call(functools.partial(kernel, blocks), out_shape=(jax.ShapeDty...  93 us
    unnamed x3, local copies, waits for them, and re-layouts  6.03 us

profile of v2, /device:TPU:31, one launch (start us, length us, event | category | flops | bytes accessed | tf_op | source)
XLA Modules:
  0.0 99.6 jit_solution(10616158066115841339)
XLA Ops:
  0.6 93.0 %mgrit_cycle.1 = (f32[1,128,1024]{2,1,0:T(8,128)}, f32[1,128,1024]{2,1,0:T(8,128)}, f32[1,1024,256]{2,1,0:T(8,128)}) custom-call(f32[128,1024]{1,0:T(8,128)} %inputs.1, f32[1,128,1024]{2,1,0:T(8,128)} %guesses.1, bf16[4,1024,1024]{2,1,0:T(8,128)(2,1)} %weights.1, f32[4,1024]{1,0:T(4,128)} %biases.1, bf16[1,128,1024]{2,1,0:T(8,128)(2,1)} %adjoint.1), custom_call_target="tpu_custom_call" | custom-call | tf_op jit(solution)/shard_map/mgrit_cycle/pallas_call | solution.py:656
  93.6 1.9 %copy.11 = f32[1,128,1024]{2,1,0:T(8,128)} copy(f32[1,128,1024]{2,1,0:T(8,128)} %get-tuple-element.6) | data formatting | bytes 1048576
  95.5 1.9 %copy.12 = f32[1,128,1024]{2,1,0:T(8,128)} copy(f32[1,128,1024]{2,1,0:T(8,128)} %get-tuple-element.7) | data formatting | bytes 1048576
  97.4 2.3 %copy.13 = f32[1,1024,256]{2,1,0:T(8,128)} copy(f32[1,1024,256]{2,1,0:T(8,128)} %get-tuple-element.8) | data formatting | bytes 2097152

commit v3 on v2

--- a/solution.py
+++ b/solution.py
@@ -12,6 +12,7 @@
 CHUNK = 16
 HALF = 64
 PIECES = 8
+VMEM_MAIN = 57 * 1024 * 1024
 
 
 def kernel(
@@ -23,7 +24,8 @@
     adjoint,
     new_out,
     coarse_out,
-    grad_out,
+    a_all,
+    d_all,
     w_v,
     state,
     guess_in,
@@ -52,9 +54,15 @@
     b_pair,
     early_send,
     early_in,
-    a_all,
+    guess_16,
+    guess_in_16,
+    relaxed_16,
+    relaxed_in_16,
+    new_v,
+    coarse_v,
+    a_own,
     d_send,
-    d_all,
+    out_sem,
     w_sem,
     half_send,
     half_recv,
@@ -101,7 +109,7 @@
     right, left = lax.rem(zed + 1, planes), lax.rem(zed + planes - 1, planes)
     across = lax.rem(zed + 2, planes)
     barrier = pltpu.get_barrier_semaphore()
-    near = (1, 2, 3, 4, 6, 8)
+    near = (1, 2, 3, 4, 6, 7, 8)
     for step in near + tuple(blocks - step for step in near):
         pl.semaphore_signal(
             barrier, inc=1, device_id=(lax.rem(me + step, blocks), zed), device_id_type=MESH
@@ -151,13 +159,29 @@
 
         lax.fori_loop(0, count, step, 0)
 
+    crosses = lax.rem(me, 2) == 1
+    came_over = lax.rem(me, 2) == 0
+    sends_wide = jnp.logical_not(crosses)
+    sends_narrow = jnp.logical_and(crosses, jnp.logical_not(is_last))
+    takes_wide = crosses
+    takes_narrow = jnp.logical_and(came_over, jnp.logical_not(is_first))
+
     def guess_hop(c):
         r = half_rows(c)
         return hop(guesses.at[0, r], guess_in.at[r], half_send.at[0, c], half_recv.at[0, c], 1)
 
-    @pl.when(jnp.logical_not(is_last))
+    def guess_hop_16(c):
+        r = half_rows(c)
+        return hop(guess_16.at[r], guess_in_16.at[r], half_send.at[0, c], half_recv.at[0, c], 1)
+
+    @pl.when(sends_wide)
     def _():
         each(halves, lambda c: guess_hop(c).start())
+
+    @pl.when(sends_narrow)
+    def _():
+        guess_16[...] = guesses[0].astype(BF16)
+        each(halves, lambda c: guess_hop_16(c).start())
 
     @pl.when(is_first)
     def _():
@@ -198,12 +222,26 @@
         r = half_rows(c)
         return hop(relaxed.at[r], relaxed_in.at[r], half_send.at[1, c], half_recv.at[1, c], 1)
 
+    def relaxed_hop_16(c):
+        r = half_rows(c)
+        return hop(
+            relaxed_16.at[r], relaxed_in_16.at[r], half_send.at[1, c], half_recv.at[1, c], 1
+        )
+
+    is_second = pos == 2
+    relaxed_wide = jnp.logical_not(jnp.logical_or(is_second, is_last))
+
     def relax_half(c):
         r = half_rows(c)
 
-        @pl.when(jnp.logical_not(is_first))
+        @pl.when(takes_wide)
         def _():
             guess_hop(c).wait_recv()
+
+        @pl.when(takes_narrow)
+        def _():
+            guess_hop_16(c).wait_recv()
+            guess_in[r, :] = guess_in_16[r, :].astype(F32)
 
         relaxed[r, :] = guess_in[r, :]
 
@@ -218,7 +256,12 @@
 
         lax.fori_loop(0, 4, layer_step, 0)
 
-        @pl.when(jnp.logical_not(is_last))
+        @pl.when(is_second)
+        def _():
+            relaxed_16[r, :] = relaxed[r, :].astype(BF16)
+            relaxed_hop_16(c).start()
+
+        @pl.when(relaxed_wide)
         def _():
             relaxed_hop(c).start()
 
@@ -228,7 +271,12 @@
     def forcing_half(c):
         r = half_rows(c)
 
-        @pl.when(jnp.logical_not(is_first))
+        @pl.when(pos == 3)
+        def _():
+            relaxed_hop_16(c).wait_recv()
+            relaxed_in[r, :] = relaxed_in_16[r, :].astype(F32)
+
+        @pl.when(jnp.logical_not(jnp.logical_or(is_first, pos == 3)))
         def _():
             relaxed_hop(c).wait_recv()
 
@@ -305,12 +353,6 @@
     each(chunks, first_sweep)
     relay_weights(5, PIECES)
 
-    @pl.when(is_pair)
-    def _():
-        each(chunks, lambda c: far_hop(0, c).wait_recv())
-        u = v_in[...]
-        own_step[...] = u + (16.0 * h) * act(u, 0)
-
     is_fourth = me == 3
 
     @pl.when(is_fourth)
@@ -334,6 +376,10 @@
         r = chunk_rows(c)
         return hop(src.at[r], final_in.at[r], final_send.at[c], final_recv.at[c], 1)
 
+    def final_row_hop(c):
+        r = chunk_rows(c)
+        return hop(solved_in.at[r], final_in.at[r], back_send.at[2, c], final_recv.at[c], -7)
+
     def final_a_hop(c):
         r = chunk_rows(c)
         return hop(solved_a.at[r], final_in.at[r], back_send.at[1, c], final_recv.at[c], -3)
@@ -341,7 +387,6 @@
     def solve_chunk(c, w_a):
         r = chunk_rows(c)
         solved_a[r, :] = w_a
-        back_hop(c).start()
         final_a_hop(c).start()
         force = update[r, :] - own_step[r, :]
         w_b = w_a + (16.0 * h) * act(w_a, 0) + force
@@ -350,9 +395,8 @@
         @pl.when(row < last_row)
         def _():
             solved_hop(c).start()
-            final_hop(c, solved).start()
-
-        coarse_out[0, r, :] = w_b - relaxed[r, :]
+
+        coarse_v[r, :] = w_b - relaxed[r, :]
 
     pair_first = jnp.logical_and(is_pair, row == 0)
 
@@ -362,6 +406,13 @@
         @pl.when(jnp.logical_not(is_first))
         def _():
             level_hop(1, c, update).wait_recv()
+
+        @pl.when(jnp.logical_and(is_pair, lax.rem(c, chunks // halves) == 0))
+        def _():
+            each(chunks // halves, lambda i: far_hop(0, c + i).wait_recv())
+            half = half_rows(c // (chunks // halves))
+            v_a = v_in[half, :]
+            own_step[half, :] = v_a + (16.0 * h) * act(v_a, 0)
 
         u = level_in[1, r, :]
         new = u + (4.0 * h) * act(u, 0) + forcing[r, :]
@@ -371,34 +422,34 @@
         def _():
             level_hop(1, c, update).start()
 
-        @pl.when(is_relay)
-        def _():
+        @pl.when(is_fourth)
+        def _():
+            step_two = below_step[r, :]
+            update[r, :] = step_two + (new - step_two)
+
+        @pl.when(is_a)
+        def _():
+            mid_hop(1, c, update).start()
+
+        @pl.when(pair_first)
+        def _():
+            far_hop(1, c).wait_recv()
+            solve_chunk(c, u_in[r, :])
+
+    each(chunks, second_sweep)
+
+    @pl.when(is_relay)
+    def _():
+        def forward_v(c):
             mid_hop(0, c, first_v).wait_recv()
             far_hop(0, c).start()
 
-        @pl.when(is_fourth)
-        def _():
-            step_two = below_step[r, :]
-            update[r, :] = step_two + (new - step_two)
-
-        @pl.when(is_a)
-        def _():
-            mid_hop(1, c, update).start()
-
-        @pl.when(pair_first)
-        def _():
-            far_hop(1, c).wait_recv()
-            solve_chunk(c, u_in[r, :])
-
-    each(chunks, second_sweep)
-
-    @pl.when(is_relay)
-    def _():
-        def forward(c):
+        def forward_u(c):
             mid_hop(1, c, update).wait_recv()
             far_hop(1, c).start()
 
-        each(chunks, forward)
+        each(chunks, forward_v)
+        each(chunks, forward_u)
 
     @pl.when(is_pair)
     def _():
@@ -416,10 +467,19 @@
             far_hop(1, c).wait_recv()
             force = u_in[r, :] - below_step[r, :]
             solved_hop(c).wait_recv()
+            final_row_hop(c).start()
             u = solved_in[r, :]
             solve_chunk(c, u + (16.0 * h) * act_pair(u) + force)
 
         each(chunks, solve_both)
+
+    def coarse_copy():
+        return pltpu.make_async_copy(coarse_v, coarse_out.at[0], out_sem.at[0, 0])
+
+    @pl.when(is_pair)
+    def _():
+        each(chunks, lambda c: back_hop(c).start())
+        coarse_copy().start()
 
     @pl.when(is_first)
     def _():
@@ -442,22 +502,12 @@
 
         state[r, :] = u + h * t
 
-    each(chunks, final_sweep)
-
-    def early_hop():
-        return hop(early_send, early_in, early_sem.at[0], early_sem.at[1], 4)
-
-    sends_early = jnp.logical_and(jnp.logical_not(is_c), me < blocks - 4)
-
-    @pl.when(sends_early)
-    def _():
-        early_send[...] = update[...].astype(BF16)
-        early_hop().start()
+    cols = d_send.shape[2]
 
     def a_hop(side, c):
         r = half_rows(c)
         return zhop(
-            a_all.at[zed, r],
+            a_own.at[r],
             a_all.at[zed, r],
             a_send.at[side, c],
             a_recv.at[side, c],
@@ -468,7 +518,7 @@
         r = half_rows(c)
         source = left if side == 0 else right
         return zhop(
-            a_all.at[source, r],
+            a_own.at[r],
             a_all.at[source, r],
             a_send.at[side, c],
             a_recv.at[side, c],
@@ -489,7 +539,7 @@
     def a_relayed(side):
         r = half_rows(side)
         return zhop(
-            a_all.at[across, r],
+            a_own.at[r],
             a_all.at[across, r],
             a_send.at[2, side],
             a_recv.at[2, side],
@@ -510,7 +560,13 @@
             d_send.at[zed, r], d_all.at[source, r], d_ssem.at[j - 1, c], d_rsem.at[j - 1, c], source
         )
 
-    cols = grad_out.shape[2]
+    def own_copies(c):
+        r = half_rows(c)
+        return (
+            pltpu.make_async_copy(new_v.at[r], new_out.at[0, r], out_sem.at[1, c]),
+            pltpu.make_async_copy(a_own.at[r], a_all.at[zed, r], out_sem.at[2, c]),
+            pltpu.make_async_copy(d_send.at[zed, r], d_all.at[zed, r], out_sem.at[3, c]),
+        )
 
     def block_half(c):
         r = half_rows(c)
@@ -523,19 +579,44 @@
         lax.fori_loop(1, 3, layer_step, 0)
         u = state[r, :]
         x = u.astype(BF16)
-        a_all[zed, r, :] = x
+        a_own[r, :] = x
         a_hop(0, c).start()
         a_hop(1, c).start()
         t = act(x, 3)
-        new_out[0, r, :] = u + h * t
         delta = (adjoint[0, r, :].astype(F32) * h * (1.0 - t * t)).astype(BF16)
         for j in range(planes):
             d_send[j, r, :] = delta[:, j * cols : (j + 1) * cols]
-        d_all[zed, r, :] = d_send[zed, r, :]
         for j in range(1, planes):
             d_hop(j, c).start()
-
-    each(halves, block_half)
+        new_v[r, :] = u + h * t
+        for copy in own_copies(c):
+            copy.start()
+
+    def turn(i, carry):
+        block = jnp.where(is_c, lax.rem(i, 2), i // halves)
+        half = jnp.where(is_c, i // 2, lax.rem(i, halves))
+
+        @pl.when(block == 0)
+        def _():
+            each(chunks // halves, lambda c: final_sweep(half * (chunks // halves) + c))
+
+        @pl.when(block == 1)
+        def _():
+            block_half(half)
+
+        return carry
+
+    lax.fori_loop(0, 2 * halves, turn, 0)
+
+    def early_hop():
+        return hop(early_send, early_in, early_sem.at[0], early_sem.at[1], 4)
+
+    sends_early = jnp.logical_and(jnp.logical_not(is_c), me < blocks - 4)
+
+    @pl.when(sends_early)
+    def _():
+        early_send[...] = update[...].astype(BF16)
+        early_hop().start()
 
     for side in range(2):
         a_came(side, side).wait_recv()
@@ -553,12 +634,16 @@
 
         below_step[...] = early_in[...].astype(F32) + (16.0 * h) * act(early_in[...], 0)
         step_two = below_step[...]
-        coarse_out[0] = step_two + (update[...] - step_two) - relaxed[...]
+        coarse_v[...] = step_two + (update[...] - step_two) - relaxed[...]
 
     @pl.when(is_a)
     def _():
         each(chunks, lambda c: back_hop(c).wait_recv())
-        coarse_out[0] = solved_back[...] - relaxed[...]
+        coarse_v[...] = solved_back[...] - relaxed[...]
+
+    @pl.when(jnp.logical_not(is_pair))
+    def _():
+        coarse_copy().start()
 
     for side in range(2):
         a_came(side, 1 - side).wait_recv()
@@ -567,21 +652,29 @@
             d_came(j, c).wait_recv()
     for side in range(2):
         a_relayed(side).wait_recv()
-    grad_out[0] = lax.dot_general(
-        a_all[...].reshape(planes * rows, a_all.shape[2]),
-        d_all[...].reshape(planes * rows, cols),
-        (((0,), (0,)), ((), ())),
-        preferred_element_type=F32,
-    )
+    coarse_copy().wait()
+    for c in range(halves):
+        for copy in own_copies(c):
+            copy.wait()
+
+    @pl.when(sends_wide)
+    def _():
+        each(halves, lambda c: guess_hop(c).wait_send())
+
+    @pl.when(sends_narrow)
+    def _():
+        each(halves, lambda c: guess_hop_16(c).wait_send())
+
+    @pl.when(is_second)
+    def _():
+        each(halves, lambda c: relaxed_hop_16(c).wait_send())
+
+    @pl.when(relaxed_wide)
+    def _():
+        each(halves, lambda c: relaxed_hop(c).wait_send())
 
     @pl.when(jnp.logical_not(is_last))
     def _():
-        def sent(c):
-            guess_hop(c).wait_send()
-            relaxed_hop(c).wait_send()
-
-        each(halves, sent)
-
         each(chunks, lambda c: first_hop(c).wait_send())
 
     @pl.when(jnp.logical_not(is_c))
@@ -625,12 +718,15 @@
 
         each(chunks, sent)
 
+    @pl.when(jnp.logical_and(is_pair, row > 0))
+    def _():
+        each(chunks, lambda c: final_row_hop(c).wait_send())
+
     @pl.when(pair_goes_on)
     def _():
         def sent(c):
             below_hop(c).wait_send()
             solved_hop(c).wait_send()
-            final_hop(c, solved).wait_send()
 
         each(chunks, sent)
 
@@ -643,6 +739,18 @@
             d_hop(j, c).wait_send()
 
 
+def finish(new, coarse, a_all, d_all, new_out, coarse_out, grad_out):
+    new_out[...] = new[...]
+    coarse_out[...] = coarse[...]
+    planes, rows, depth = a_all.shape
+    grad_out[0] = lax.dot_general(
+        a_all[...].reshape(planes * rows, depth),
+        d_all[...].reshape(planes * rows, d_all.shape[2]),
+        (((0,), (0,)), ((), ())),
+        preferred_element_type=F32,
+    )
+
+
 def solution(mesh):
     blocks, planes = mesh.shape["layer"], mesh.shape["dp"]
 
@@ -653,15 +761,17 @@
         whole = pltpu.VMEM((rows, width), F32)
         dma = pltpu.SemaphoreType.DMA
         vmem = pl.BlockSpec(memory_space=pltpu.VMEM)
-        return pl.pallas_call(
+        anywhere = pl.BlockSpec(memory_space=pl.ANY)
+        new, coarse, a_all, d_all = pl.pallas_call(
             functools.partial(kernel, blocks),
             out_shape=(
                 jax.ShapeDtypeStruct((1, rows, width), F32),
                 jax.ShapeDtypeStruct((1, rows, width), F32),
-                jax.ShapeDtypeStruct((1, width, cols), F32),
+                jax.ShapeDtypeStruct((planes, rows, width), BF16),
+                jax.ShapeDtypeStruct((planes, rows, cols), BF16),
             ),
-            in_specs=[vmem, vmem, pl.BlockSpec(memory_space=pl.ANY), vmem, vmem],
-            out_specs=(vmem, vmem, vmem),
+            in_specs=[vmem, vmem, anywhere, vmem, vmem],
+            out_specs=(anywhere,) * 4,
             scratch_shapes=[
                 pltpu.VMEM((4, width, width), BF16),
                 whole,
@@ -691,9 +801,15 @@
                 pltpu.VMEM((8, width), F32),
                 pltpu.VMEM((rows, width), BF16),
                 pltpu.VMEM((rows, width), BF16),
-                pltpu.VMEM((planes, rows, width), BF16),
+                pltpu.VMEM((rows, width), BF16),
+                pltpu.VMEM((rows, width), BF16),
+                pltpu.VMEM((rows, width), BF16),
+                pltpu.VMEM((rows, width), BF16),
+                whole,
+                whole,
+                pltpu.VMEM((rows, width), BF16),
                 pltpu.VMEM((planes, rows, cols), BF16),
-                pltpu.VMEM((planes, rows, cols), BF16),
+                dma((4, halves)),
                 dma((4,)),
                 dma((2, halves)),
                 dma((2, halves)),
@@ -705,7 +821,7 @@
                 dma((chunks,)),
                 dma((chunks,)),
                 dma((chunks,)),
-                dma((2, chunks)),
+                dma((3, chunks)),
                 dma((chunks,)),
                 dma((2, chunks)),
                 dma((2, chunks)),
@@ -723,10 +839,30 @@
                 dma((planes - 1, halves)),
             ],
             compiler_params=pltpu.CompilerParams(
-                collective_id=0, has_side_effects=True, vmem_limit_bytes=60 * 1024 * 1024
+                collective_id=0, has_side_effects=True, vmem_limit_bytes=VMEM_MAIN
             ),
             name="mgrit_cycle",
         )(inputs, guesses, weights, biases, adjoint)
+        parts = 4
+        slab = pl.BlockSpec((1, rows // parts, width), lambda i: (0, i, 0))
+        return pl.pallas_call(
+            finish,
+            grid=(parts,),
+            out_shape=(
+                jax.ShapeDtypeStruct((1, rows, width), F32),
+                jax.ShapeDtypeStruct((1, rows, width), F32),
+                jax.ShapeDtypeStruct((1, width, cols), F32),
+            ),
+            in_specs=[
+                slab,
+                slab,
+                pl.BlockSpec((planes, rows, width // parts), lambda i: (0, 0, i)),
+                pl.BlockSpec((planes, rows, cols), lambda i: (0, 0, 0)),
+            ],
+            out_specs=(slab, slab, pl.BlockSpec((1, width // parts, cols), lambda i: (0, i, 0))),
+            compiler_params=pltpu.CompilerParams(vmem_limit_bytes=16 * 1024 * 1024),
+            name="results",
+        )(new, coarse, a_all, d_all)
 
     return jax.shard_map(
         body,

time: 99.9 us -> 91.6 us (0.917); the launches traced: 99.6 us -> 89.8 us
  Pallas kernels: 93 us -> 84.9 us
  local copies, waits for them, and re-layouts: 6.03 us -> 4.25 us
    pallas_call x1, Pallas kernels: 93 us -> 82.6 us  [body(): pl.pallas_call(functools.partial(kernel, blocks), out_shape=(jax.ShapeDty...]
    pallas_call x0 -> x1, Pallas kernels: none -> 2.37 us  [body(): pl.pallas_call(finish, grid=(parts,), out_shape=(jax.ShapeDtypeStruct((1,...]
    unnamed x3 -> x8, local copies, waits for them, and re-layouts: 6.03 us -> 4.25 us
where the time goes in v3:
time: 91.6 us; the launch traced here: 89.8 us
  Pallas kernels  84.9 us (93%)
  local copies, waits for them, and re-layouts  4.25 us (5%)
    pallas_call x1, Pallas kernels, body(): pl.pallas_call(functools.partial(kernel, blocks), out_shape=(jax.ShapeDty...  82.6 us
    unnamed x8, local copies, waits for them, and re-layouts  4.25 us
    pallas_call x1, Pallas kernels, body(): pl.pallas_call(finish, grid=(parts,), out_shape=(jax.ShapeDtypeStruct((1,...  2.37 us

profile of v3, /device:TPU:31, one launch (start us, length us, event | category | flops | bytes accessed | tf_op | source)
XLA Modules:
  0.0 89.8 jit_solution(13044342955783946220)
XLA Ops:
  0.6 82.6 %mgrit_cycle.1 = (f32[1,128,1024]{2,1,0:T(8,128)}, f32[1,128,1024]{2,1,0:T(8,128)}, bf16[4,128,1024]{2,1,0:T(8,128)(2,1)}, bf16[4,128,256]{2,1,0:T(8,128)(2,1)}) custom-call(f32[128,1024]{1,0:T(8,128)} %inputs.1, f32[1,128,1024]{2,1,0:T(8,128)} %guesses.1, bf16[4,1024,1024]{2,1,0:T(8,128)(2,1)} %weights.1, f32[4,1024]{1,0:T(4,128)} %biases.1, ...), custom_call_target="tpu_custom_call" | custom-call | tf_op jit(solution)/shard_map/mgrit_cycle/pallas_call | solution.py:765
  83.2 0.0 copy-start
  83.2 1.2 %copy-done = bf16[4,128,1024]{2,1,0:T(8,128)(2,1)S(1)} copy-done((bf16[4,128,1024]{2,1,0:T(8,128)(2,1)S(1)}, bf16[4,128,1024]{2,1,0:T(8,128)(2,1)}, u32[]{:S(2)}) %copy-start) | copy-done | bytes 1048600
  84.4 0.0 copy-start.1
  84.4 1.0 %copy-done.1 = f32[1,128,1024]{2,1,0:T(8,128)S(1)} copy-done((f32[1,128,1024]{2,1,0:T(8,128)S(1)}, f32[1,128,1024]{2,1,0:T(8,128)}, u32[]{:S(2)}) %copy-start.1) | copy-done | bytes 524312
  85.5 0.0 copy-start.2
  85.5 1.0 %copy-done.2 = f32[1,128,1024]{2,1,0:T(8,128)S(1)} copy-done((f32[1,128,1024]{2,1,0:T(8,128)S(1)}, f32[1,128,1024]{2,1,0:T(8,128)}, u32[]{:S(2)}) %copy-start.2) | copy-done | bytes 524312
  86.5 0.0 copy-start.3
  86.5 0.9 %copy-done.3 = bf16[4,128,256]{2,1,0:T(8,128)(2,1)S(1)} copy-done((bf16[4,128,256]{2,1,0:T(8,128)(2,1)S(1)}, bf16[4,128,256]{2,1,0:T(8,128)(2,1)}, u32[]{:S(2)}) %copy-start.3) | copy-done | bytes 262168
  87.5 2.4 %results.1 = (f32[1,128,1024]{2,1,0:T(8,128)}, f32[1,128,1024]{2,1,0:T(8,128)}, f32[1,1024,256]{2,1,0:T(8,128)}) custom-call(f32[1,128,1024]{2,1,0:T(8,128)S(1)} %copy-done.1, f32[1,128,1024]{2,1,0:T(8,128)S(1)} %copy-done.2, bf16[4,128,1024]{2,1,0:T(8,128)(2,1)S(1)} %copy-done, bf16[4,128,256]{2,1,0:T(8,128)(2,1)S(1)} %copy-done.3), custom_call_target="tpu_custom_call" | custom-call | tf_op jit(solution)/shard_map/results/pallas_call | solution.py:848
Async XLA Ops:
  83.2 1.2 %copy-start = (bf16[4,128,1024]{2,1,0:T(8,128)(2,1)S(1)}, bf16[4,128,1024]{2,1,0:T(8,128)(2,1)}, u32[]{:S(2)}) copy-start(bf16[4,128,1024]{2,1,0:T(8,128)(2,1)} %get-tuple-element.9.a_all) | copy-start | bytes 3145732
  84.4 1.0 %copy-start.1 = (f32[1,128,1024]{2,1,0:T(8,128)S(1)}, f32[1,128,1024]{2,1,0:T(8,128)}, u32[]{:S(2)}) copy-start(f32[1,128,1024]{2,1,0:T(8,128)} %get-tuple-element.7.new) | copy-start | bytes 1572868
  85.5 1.0 %copy-start.2 = (f32[1,128,1024]{2,1,0:T(8,128)S(1)}, f32[1,128,1024]{2,1,0:T(8,128)}, u32[]{:S(2)}) copy-start(f32[1,128,1024]{2,1,0:T(8,128)} %get-tuple-element.8.coarse) | copy-start | bytes 1572868
  86.5 0.9 %copy-start.3 = (bf16[4,128,256]{2,1,0:T(8,128)(2,1)S(1)}, bf16[4,128,256]{2,1,0:T(8,128)(2,1)}, u32[]{:S(2)}) copy-start(bf16[4,128,256]{2,1,0:T(8,128)(2,1)} %get-tuple-element.10.d_all) | copy-start | bytes 786436

commit v4 on v3

--- a/solution.py
+++ b/solution.py
@@ -12,20 +12,24 @@
 CHUNK = 16
 HALF = 64
 PIECES = 8
-VMEM_MAIN = 57 * 1024 * 1024
+VMEM_MAIN = 40 * 1024 * 1024
 
 
 def kernel(
     blocks,
-    inputs,
-    guesses,
+    inputs_h,
+    guesses_h,
     weights,
-    biases,
-    adjoint,
+    biases_h,
+    adjoint_h,
     new_out,
     coarse_out,
     a_all,
     d_all,
+    inputs,
+    guesses,
+    biases,
+    adjoint,
     w_v,
     state,
     guess_in,
@@ -44,11 +48,8 @@
     solved_back,
     final_v,
     final_in,
-    v_mid,
     v_in,
-    u_mid,
     u_in,
-    w_mid,
     w_pair,
     b_send,
     b_pair,
@@ -63,6 +64,7 @@
     a_own,
     d_send,
     out_sem,
+    in_sem,
     w_sem,
     half_send,
     half_recv,
@@ -76,12 +78,8 @@
     final_recv,
     back_send,
     back_recv,
-    mid_send,
-    mid_recv,
     far_send,
     far_recv,
-    wmid_send,
-    wmid_recv,
     wfar_send,
     wfar_recv,
     b_sem,
@@ -91,7 +89,7 @@
     d_ssem,
     d_rsem,
 ):
-    rows = inputs.shape[0]
+    rows = inputs_h.shape[0]
     chunks, halves = rows // CHUNK, rows // HALF
     h = 4.0 / (4 * blocks)
     me, zed = lax.axis_index("layer"), lax.axis_index("dp")
@@ -100,16 +98,26 @@
     is_first, is_last = me == 0, me == blocks - 1
     is_c = pos == 0
     seat, row = lax.rem(me, 8), me // 8
-    is_a, is_pair, is_relay = seat == 3, seat == 7, seat == 1
+    is_a, is_pair = seat == 3, seat == 7
     last_row = blocks // 8 - 1
 
-    for layer in range(4):
-        pltpu.make_async_copy(weights.at[layer], w_v.at[layer], w_sem.at[layer]).start()
+    arrivals = [
+        pltpu.make_async_copy(src, dst, in_sem.at[i])
+        for i, (src, dst) in enumerate(
+            ((guesses_h, guesses), (biases_h, biases), (inputs_h, inputs), (adjoint_h, adjoint))
+        )
+    ]
+    def weight_copy(layer):
+        return pltpu.make_async_copy(weights.at[layer], w_v.at[layer], w_sem.at[layer])
+
+    for copy in arrivals[:3]:
+        copy.start()
+    weight_copy(0).start()
 
     right, left = lax.rem(zed + 1, planes), lax.rem(zed + planes - 1, planes)
     across = lax.rem(zed + 2, planes)
     barrier = pltpu.get_barrier_semaphore()
-    near = (1, 2, 3, 4, 6, 7, 8)
+    near = (1, 3, 4, 7, 8)
     for step in near + tuple(blocks - step for step in near):
         pl.semaphore_signal(
             barrier, inc=1, device_id=(lax.rem(me + step, blocks), zed), device_id_type=MESH
@@ -159,6 +167,10 @@
 
         lax.fori_loop(0, count, step, 0)
 
+    for copy in arrivals[:3]:
+        copy.wait()
+    weight_copy(1).start()
+
     crosses = lax.rem(me, 2) == 1
     came_over = lax.rem(me, 2) == 0
     sends_wide = jnp.logical_not(crosses)
@@ -192,32 +204,19 @@
         depth = weights.shape[1] // PIECES
         return pl.ds(pl.multiple_of(i * depth, depth), depth)
 
-    def weight_mid(i):
-        r = piece_rows(i)
-        return hop(weights.at[0, r], w_mid.at[r], wmid_send.at[i], wmid_recv.at[i], -2)
-
     def weight_far(i):
         r = piece_rows(i)
-        return hop(w_mid.at[r], w_pair.at[r], wfar_send.at[i], wfar_recv.at[i], 6)
+        return hop(weights.at[0, r], w_pair.at[r], wfar_send.at[i], wfar_recv.at[i], 4)
 
     def bias_hop():
         return hop(b_send, b_pair, b_sem.at[0], b_sem.at[1], 4)
 
     @pl.when(is_a)
     def _():
-        each(PIECES, lambda i: weight_mid(i).start())
+        each(PIECES, lambda i: weight_far(i).start())
         b_send[...] = jnp.broadcast_to(biases[0:1, :], b_send.shape)
         bias_hop().start()
 
-    def relay_weights(start, stop):
-        @pl.when(is_relay)
-        def _():
-            def forward(i):
-                weight_mid(start + i).wait_recv()
-                weight_far(start + i).start()
-
-            each(stop - start, forward)
-
     def relaxed_hop(c):
         r = half_rows(c)
         return hop(relaxed.at[r], relaxed_in.at[r], half_send.at[1, c], half_recv.at[1, c], 1)
@@ -231,9 +230,7 @@
     is_second = pos == 2
     relaxed_wide = jnp.logical_not(jnp.logical_or(is_second, is_last))
 
-    def relax_half(c):
-        r = half_rows(c)
-
+    def await_guess(c):
         @pl.when(takes_wide)
         def _():
             guess_hop(c).wait_recv()
@@ -241,32 +238,60 @@
         @pl.when(takes_narrow)
         def _():
             guess_hop_16(c).wait_recv()
-            guess_in[r, :] = guess_in_16[r, :].astype(F32)
-
-        relaxed[r, :] = guess_in[r, :]
-
-        def layer_step(layer, carry):
-            @pl.when(c == 0)
-            def _():
-                pltpu.make_async_copy(weights.at[layer], w_v.at[layer], w_sem.at[layer]).wait()
-
-            u = relaxed[r, :]
-            relaxed[r, :] = u + h * act(u, layer)
-            return carry
-
-        lax.fori_loop(0, 4, layer_step, 0)
-
-        @pl.when(is_second)
-        def _():
-            relaxed_16[r, :] = relaxed[r, :].astype(BF16)
-            relaxed_hop_16(c).start()
-
-        @pl.when(relaxed_wide)
-        def _():
-            relaxed_hop(c).start()
-
-    each(halves, relax_half)
-    relay_weights(0, 2)
+
+    each(halves, await_guess)
+
+    @pl.when(takes_narrow)
+    def _():
+        guess_in[...] = guess_in_16[...].astype(F32)
+
+    relaxed[...] = guess_in[...]
+
+    def relax_layer(layer, carry):
+        weight_copy(layer).wait()
+
+        @pl.when(layer < 2)
+        def _():
+            weight_copy(layer + 2).start()
+
+        u = relaxed[...]
+        relaxed[...] = u + h * act(u, layer)
+        return carry
+
+    lax.fori_loop(0, 4, relax_layer, 0)
+    arrivals[3].start()
+
+    @pl.when(is_second)
+    def _():
+        relaxed_16[...] = relaxed[...].astype(BF16)
+        each(halves, lambda c: relaxed_hop_16(c).start())
+
+    @pl.when(relaxed_wide)
+    def _():
+        each(halves, lambda c: relaxed_hop(c).start())
+
+    slot = jnp.where(is_c, 1, 0)
+
+    def level_hop(sweep, c, src):
+        r = chunk_rows(c)
+        return hop(
+            src.at[r], level_in.at[sweep, r], level_send.at[sweep, c], level_recv.at[sweep, c], 1
+        )
+
+    def first_hop(c):
+        r = chunk_rows(c)
+        return hop(
+            first_v.at[r], level_in.at[slot, r], level_send.at[0, c], level_recv.at[slot, c], 1
+        )
+
+    def below_hop(c):
+        r = chunk_rows(c)
+        return hop(first_v.at[r], below_in.at[r], below_send.at[c], below_recv.at[c], 8)
+
+    def far_hop(kind, c):
+        r = chunk_rows(c)
+        src, dst = ((first_v, v_in), (update, u_in))[kind]
+        return hop(src.at[r], dst.at[r], far_send.at[kind, c], far_recv.at[kind, c], 4)
 
     def forcing_half(c):
         r = half_rows(c)
@@ -296,47 +321,20 @@
         forcing[r, :] = force
         first_v[r, :] = first_v[r, :] + force
 
+        @pl.when(pos == 1)
+        def _():
+            each(chunks // halves, lambda i: first_hop(c * (chunks // halves) + i).start())
+
     each(halves, forcing_half)
-    relay_weights(2, 5)
-
-    slot = jnp.where(is_c, 1, 0)
-
-    def level_hop(sweep, c, src):
-        r = chunk_rows(c)
-        return hop(
-            src.at[r], level_in.at[sweep, r], level_send.at[sweep, c], level_recv.at[sweep, c], 1
-        )
-
-    def first_hop(c):
-        r = chunk_rows(c)
-        return hop(
-            first_v.at[r], level_in.at[slot, r], level_send.at[0, c], level_recv.at[slot, c], 1
-        )
-
-    def below_hop(c):
-        r = chunk_rows(c)
-        return hop(first_v.at[r], below_in.at[r], below_send.at[c], below_recv.at[c], 8)
-
-    def mid_hop(kind, c, src):
-        r = chunk_rows(c)
-        dst = (v_mid, u_mid)[kind]
-        return hop(src.at[r], dst.at[r], mid_send.at[kind, c], mid_recv.at[kind, c], -2)
-
-    def far_hop(kind, c):
-        r = chunk_rows(c)
-        src, dst = ((v_mid, v_in), (u_mid, u_in))[kind]
-        return hop(src.at[r], dst.at[r], far_send.at[kind, c], far_recv.at[kind, c], 6)
 
     pair_goes_on = jnp.logical_and(is_pair, row < last_row)
 
     def first_sweep(c):
         r = chunk_rows(c)
 
-        @pl.when(pos != 1)
-        def _():
-            level_hop(0, c, first_v).wait_recv()
-            u = level_in[0, r, :]
-            first_v[r, :] = u + (4.0 * h) * act(u, 0) + forcing[r, :]
+        level_hop(0, c, first_v).wait_recv()
+        u = level_in[0, r, :]
+        first_v[r, :] = u + (4.0 * h) * act(u, 0) + forcing[r, :]
 
         @pl.when(jnp.logical_not(is_last))
         def _():
@@ -344,14 +342,15 @@
 
         @pl.when(is_a)
         def _():
-            mid_hop(0, c, first_v).start()
+            far_hop(0, c).start()
 
         @pl.when(pair_goes_on)
         def _():
             below_hop(c).start()
 
-    each(chunks, first_sweep)
-    relay_weights(5, PIECES)
+    @pl.when(pos != 1)
+    def _():
+        each(chunks, first_sweep)
 
     is_fourth = me == 3
 
@@ -429,7 +428,7 @@
 
         @pl.when(is_a)
         def _():
-            mid_hop(1, c, update).start()
+            far_hop(1, c).start()
 
         @pl.when(pair_first)
         def _():
@@ -437,19 +436,6 @@
             solve_chunk(c, u_in[r, :])
 
     each(chunks, second_sweep)
-
-    @pl.when(is_relay)
-    def _():
-        def forward_v(c):
-            mid_hop(0, c, first_v).wait_recv()
-            far_hop(0, c).start()
-
-        def forward_u(c):
-            mid_hop(1, c, update).wait_recv()
-            far_hop(1, c).start()
-
-        each(chunks, forward_v)
-        each(chunks, forward_u)
 
     @pl.when(is_pair)
     def _():
@@ -606,6 +592,7 @@
 
         return carry
 
+    arrivals[3].wait()
     lax.fori_loop(0, 2 * halves, turn, 0)
 
     def early_hop():
@@ -691,18 +678,8 @@
 
     @pl.when(is_a)
     def _():
-        each(PIECES, lambda i: weight_mid(i).wait_send())
+        each(PIECES, lambda i: weight_far(i).wait_send())
         bias_hop().wait_send()
-
-        def sent(c):
-            mid_hop(0, c, first_v).wait_send()
-            mid_hop(1, c, update).wait_send()
-
-        each(chunks, sent)
-
-    @pl.when(is_relay)
-    def _():
-        each(PIECES, lambda i: weight_far(i).wait_send())
 
         def sent(c):
             far_hop(0, c).wait_send()
@@ -760,8 +737,11 @@
         chunks, halves = rows // CHUNK, rows // HALF
         whole = pltpu.VMEM((rows, width), F32)
         dma = pltpu.SemaphoreType.DMA
-        vmem = pl.BlockSpec(memory_space=pltpu.VMEM)
         anywhere = pl.BlockSpec(memory_space=pl.ANY)
+        held = [
+            pltpu.with_memory_space_constraint(x, pltpu.HBM)
+            for x in (inputs, guesses, weights, biases, adjoint)
+        ]
         new, coarse, a_all, d_all = pl.pallas_call(
             functools.partial(kernel, blocks),
             out_shape=(
@@ -770,9 +750,13 @@
                 jax.ShapeDtypeStruct((planes, rows, width), BF16),
                 jax.ShapeDtypeStruct((planes, rows, cols), BF16),
             ),
-            in_specs=[vmem, vmem, anywhere, vmem, vmem],
+            in_specs=[pl.BlockSpec(memory_space=pltpu.HBM)] * 5,
             out_specs=(anywhere,) * 4,
             scratch_shapes=[
+                pltpu.VMEM((rows, width), F32),
+                pltpu.VMEM((1, rows, width), F32),
+                pltpu.VMEM((4, width), F32),
+                pltpu.VMEM((1, rows, width), BF16),
                 pltpu.VMEM((4, width, width), BF16),
                 whole,
                 whole,
@@ -793,9 +777,6 @@
                 whole,
                 whole,
                 whole,
-                whole,
-                whole,
-                pltpu.VMEM((width, width), BF16),
                 pltpu.VMEM((width, width), BF16),
                 pltpu.VMEM((8, width), F32),
                 pltpu.VMEM((8, width), F32),
@@ -810,6 +791,7 @@
                 pltpu.VMEM((rows, width), BF16),
                 pltpu.VMEM((planes, rows, cols), BF16),
                 dma((4, halves)),
+                dma((4,)),
                 dma((4,)),
                 dma((2, halves)),
                 dma((2, halves)),
@@ -825,10 +807,6 @@
                 dma((chunks,)),
                 dma((2, chunks)),
                 dma((2, chunks)),
-                dma((2, chunks)),
-                dma((2, chunks)),
-                dma((PIECES,)),
-                dma((PIECES,)),
                 dma((PIECES,)),
                 dma((PIECES,)),
                 dma((2,)),
@@ -842,7 +820,7 @@
                 collective_id=0, has_side_effects=True, vmem_limit_bytes=VMEM_MAIN
             ),
             name="mgrit_cycle",
-        )(inputs, guesses, weights, biases, adjoint)
+        )(*held)
         parts = 4
         slab = pl.BlockSpec((1, rows // parts, width), lambda i: (0, i, 0))
         return pl.pallas_call(

time: 91.6 us -> 79.7 us (0.87)
  Pallas kernels: 84.9 us -> 77.5 us
  local copies, waits for them, and re-layouts: 4.25 us -> 0 us
    pallas_call x1, Pallas kernels: 82.6 us -> 75.1 us  [body(): pl.pallas_call(functools.partial(kernel, blocks), out_shape=(jax.ShapeDty...]
    unnamed x8 -> x0, local copies, waits for them, and re-layouts: 4.25 us -> none
where the time goes in v4:
time: 79.7 us; the launch traced here: 78.1 us
  Pallas kernels  77.5 us (97%)
    pallas_call x1, Pallas kernels, body(): pl.pallas_call(functools.partial(kernel, blocks), out_shape=(jax.ShapeDty...  75.1 us
    pallas_call x1, Pallas kernels, body(): pl.pallas_call(finish, grid=(parts,), out_shape=(jax.ShapeDtypeStruct((1,...  2.38 us

profile of v4, /device:TPU:31, one launch (start us, length us, event | category | flops | bytes accessed | tf_op | source)
XLA Modules:
  0.0 78.1 jit_solution(17336238845904961163)
XLA Ops:
  0.6 75.1 %mgrit_cycle.1 = (f32[1,128,1024]{2,1,0:T(8,128)S(1)}, f32[1,128,1024]{2,1,0:T(8,128)S(1)}, bf16[4,128,1024]{2,1,0:T(8,128)(2,1)S(1)}, bf16[4,128,256]{2,1,0:T(8,128)(2,1)S(1)}) custom-call(f32[128,1024]{1,0:T(8,128)} %inputs_h.1, f32[1,128,1024]{2,1,0:T(8,128)} %guesses_h.1, bf16[4,1024,1024]{2,1,0:T(8,128)(2,1)} %weights.1, f32[4,1024]{1,0:T(4,128)} %biases_h.1, ...), custom_call_target="tpu_custom_call" | custom-call | tf_op jit(solution)/shard_map/mgrit_cycle/pallas_call | solution.py:745
  75.8 2.4 %results.1 = (f32[1,128,1024]{2,1,0:T(8,128)}, f32[1,128,1024]{2,1,0:T(8,128)}, f32[1,1024,256]{2,1,0:T(8,128)}) custom-call(f32[1,128,1024]{2,1,0:T(8,128)S(1)} %get-tuple-element.7.new, f32[1,128,1024]{2,1,0:T(8,128)S(1)} %get-tuple-element.8.coarse, bf16[4,128,1024]{2,1,0:T(8,128)(2,1)S(1)} %get-tuple-element.9.a_all, ...), custom_call_target="tpu_custom_call" | custom-call | tf_op jit(solution)/shard_map/results/pallas_call | solution.py:826

commit v5 on v4

--- a/solution.py
+++ b/solution.py
@@ -24,8 +24,7 @@
     adjoint_h,
     new_out,
     coarse_out,
-    a_all,
-    d_all,
+    grad_out,
     inputs,
     guesses,
     biases,
@@ -59,11 +58,9 @@
     guess_in_16,
     relaxed_16,
     relaxed_in_16,
-    new_v,
-    coarse_v,
     a_own,
-    d_send,
-    out_sem,
+    a_all,
+    adjoint_all,
     in_sem,
     w_sem,
     half_send,
@@ -86,8 +83,8 @@
     early_sem,
     a_send,
     a_recv,
-    d_ssem,
-    d_rsem,
+    adj_send,
+    adj_recv,
 ):
     rows = inputs_h.shape[0]
     chunks, halves = rows // CHUNK, rows // HALF
@@ -117,13 +114,18 @@
     right, left = lax.rem(zed + 1, planes), lax.rem(zed + planes - 1, planes)
     across = lax.rem(zed + 2, planes)
     barrier = pltpu.get_barrier_semaphore()
-    near = (1, 3, 4, 7, 8)
+    near = (1, 3, 4, 8)
     for step in near + tuple(blocks - step for step in near):
         pl.semaphore_signal(
             barrier, inc=1, device_id=(lax.rem(me + step, blocks), zed), device_id_type=MESH
         )
     for other in (right, left, across):
         pl.semaphore_signal(barrier, inc=1, device_id=(me, other), device_id_type=MESH)
+    for copy in arrivals[:3]:
+        copy.wait()
+    for layer in range(1, 4):
+        weight_copy(layer).start()
+    arrivals[3].start()
     pl.semaphore_wait(barrier, 2 * len(near) + 3)
 
     def hop(src, dst, send_sem, recv_sem, by):
@@ -167,10 +169,6 @@
 
         lax.fori_loop(0, count, step, 0)
 
-    for copy in arrivals[:3]:
-        copy.wait()
-    weight_copy(1).start()
-
     crosses = lax.rem(me, 2) == 1
     came_over = lax.rem(me, 2) == 0
     sends_wide = jnp.logical_not(crosses)
@@ -211,7 +209,10 @@
     def bias_hop():
         return hop(b_send, b_pair, b_sem.at[0], b_sem.at[1], 4)
 
-    @pl.when(is_a)
+    weight_leaves = jnp.logical_and(is_a, row > 0)
+    weight_comes = jnp.logical_and(is_pair, row > 0)
+
+    @pl.when(weight_leaves)
     def _():
         each(PIECES, lambda i: weight_far(i).start())
         b_send[...] = jnp.broadcast_to(biases[0:1, :], b_send.shape)
@@ -249,17 +250,31 @@
 
     def relax_layer(layer, carry):
         weight_copy(layer).wait()
-
-        @pl.when(layer < 2)
-        def _():
-            weight_copy(layer + 2).start()
-
         u = relaxed[...]
         relaxed[...] = u + h * act(u, layer)
         return carry
 
     lax.fori_loop(0, 4, relax_layer, 0)
-    arrivals[3].start()
+
+    cols = adjoint_all.shape[2]
+    own_cols = pl.ds(pl.multiple_of(zed * cols, cols), cols)
+
+    def adjoint_hop(j):
+        to = lax.rem(zed + j, planes)
+        to_cols = pl.ds(pl.multiple_of(to * cols, cols), cols)
+        return zhop(
+            adjoint.at[0, :, to_cols], adjoint_all.at[zed], adj_send.at[j - 1], adj_recv.at[j - 1], to
+        )
+
+    def adjoint_came(j):
+        source = lax.rem(zed + planes - j, planes)
+        return zhop(
+            adjoint.at[0, :, own_cols],
+            adjoint_all.at[source],
+            adj_send.at[j - 1],
+            adj_recv.at[j - 1],
+            source,
+        )
 
     @pl.when(is_second)
     def _():
@@ -292,6 +307,11 @@
         r = chunk_rows(c)
         src, dst = ((first_v, v_in), (update, u_in))[kind]
         return hop(src.at[r], dst.at[r], far_send.at[kind, c], far_recv.at[kind, c], 4)
+
+    arrivals[3].wait()
+    for j in range(1, planes):
+        adjoint_hop(j).start()
+    adjoint_all[zed] = adjoint[0, :, own_cols]
 
     def forcing_half(c):
         r = half_rows(c)
@@ -375,10 +395,6 @@
         r = chunk_rows(c)
         return hop(src.at[r], final_in.at[r], final_send.at[c], final_recv.at[c], 1)
 
-    def final_row_hop(c):
-        r = chunk_rows(c)
-        return hop(solved_in.at[r], final_in.at[r], back_send.at[2, c], final_recv.at[c], -7)
-
     def final_a_hop(c):
         r = chunk_rows(c)
         return hop(solved_a.at[r], final_in.at[r], back_send.at[1, c], final_recv.at[c], -3)
@@ -387,15 +403,15 @@
         r = chunk_rows(c)
         solved_a[r, :] = w_a
         final_a_hop(c).start()
-        force = update[r, :] - own_step[r, :]
-        w_b = w_a + (16.0 * h) * act(w_a, 0) + force
-        solved[r, :] = w_b
 
         @pl.when(row < last_row)
         def _():
+            force = update[r, :] - own_step[r, :]
+            w_b = w_a + (16.0 * h) * act(w_a, 0) + force
+            solved[r, :] = w_b
             solved_hop(c).start()
-
-        coarse_v[r, :] = w_b - relaxed[r, :]
+            final_hop(c, solved).start()
+            coarse_out[0, r, :] = w_b - relaxed[r, :]
 
     pair_first = jnp.logical_and(is_pair, row == 0)
 
@@ -437,13 +453,10 @@
 
     each(chunks, second_sweep)
 
-    @pl.when(is_pair)
+    @pl.when(weight_comes)
     def _():
         each(PIECES, lambda i: weight_far(i).wait_recv())
         bias_hop().wait_recv()
-
-    @pl.when(jnp.logical_and(is_pair, row > 0))
-    def _():
         each(chunks, lambda c: below_hop(c).wait_recv())
         u = below_in[...]
         below_step[...] = u + (16.0 * h) * act_pair(u)
@@ -453,19 +466,20 @@
             far_hop(1, c).wait_recv()
             force = u_in[r, :] - below_step[r, :]
             solved_hop(c).wait_recv()
-            final_row_hop(c).start()
             u = solved_in[r, :]
             solve_chunk(c, u + (16.0 * h) * act_pair(u) + force)
 
         each(chunks, solve_both)
 
-    def coarse_copy():
-        return pltpu.make_async_copy(coarse_v, coarse_out.at[0], out_sem.at[0, 0])
+    @pl.when(is_last)
+    def _():
+        w_a = solved_a[...]
+        w_b = w_a + (16.0 * h) * act(w_a, 0) + (update[...] - own_step[...])
+        coarse_out[0] = w_b - relaxed[...]
 
     @pl.when(is_pair)
     def _():
         each(chunks, lambda c: back_hop(c).start())
-        coarse_copy().start()
 
     @pl.when(is_first)
     def _():
@@ -487,8 +501,6 @@
             final_hop(c, final_v).start()
 
         state[r, :] = u + h * t
-
-    cols = d_send.shape[2]
 
     def a_hop(side, c):
         r = half_rows(c)
@@ -532,28 +544,6 @@
             right if side == 0 else left,
         )
 
-    def d_hop(j, c):
-        r = half_rows(c)
-        to = lax.rem(zed + j, planes)
-        return zhop(
-            d_send.at[to, r], d_all.at[zed, r], d_ssem.at[j - 1, c], d_rsem.at[j - 1, c], to
-        )
-
-    def d_came(j, c):
-        r = half_rows(c)
-        source = lax.rem(zed + planes - j, planes)
-        return zhop(
-            d_send.at[zed, r], d_all.at[source, r], d_ssem.at[j - 1, c], d_rsem.at[j - 1, c], source
-        )
-
-    def own_copies(c):
-        r = half_rows(c)
-        return (
-            pltpu.make_async_copy(new_v.at[r], new_out.at[0, r], out_sem.at[1, c]),
-            pltpu.make_async_copy(a_own.at[r], a_all.at[zed, r], out_sem.at[2, c]),
-            pltpu.make_async_copy(d_send.at[zed, r], d_all.at[zed, r], out_sem.at[3, c]),
-        )
-
     def block_half(c):
         r = half_rows(c)
 
@@ -569,31 +559,13 @@
         a_hop(0, c).start()
         a_hop(1, c).start()
         t = act(x, 3)
-        delta = (adjoint[0, r, :].astype(F32) * h * (1.0 - t * t)).astype(BF16)
-        for j in range(planes):
-            d_send[j, r, :] = delta[:, j * cols : (j + 1) * cols]
-        for j in range(1, planes):
-            d_hop(j, c).start()
-        new_v[r, :] = u + h * t
-        for copy in own_copies(c):
-            copy.start()
-
-    def turn(i, carry):
-        block = jnp.where(is_c, lax.rem(i, 2), i // halves)
-        half = jnp.where(is_c, i // 2, lax.rem(i, halves))
-
-        @pl.when(block == 0)
-        def _():
-            each(chunks // halves, lambda c: final_sweep(half * (chunks // halves) + c))
-
-        @pl.when(block == 1)
-        def _():
-            block_half(half)
-
-        return carry
-
-    arrivals[3].wait()
-    lax.fori_loop(0, 2 * halves, turn, 0)
+        new_out[0, r, :] = u + h * t
+
+    def final_half(half):
+        each(chunks // halves, lambda c: final_sweep(half * (chunks // halves) + c))
+        block_half(half)
+
+    each(halves, final_half)
 
     def early_hop():
         return hop(early_send, early_in, early_sem.at[0], early_sem.at[1], 4)
@@ -621,29 +593,29 @@
 
         below_step[...] = early_in[...].astype(F32) + (16.0 * h) * act(early_in[...], 0)
         step_two = below_step[...]
-        coarse_v[...] = step_two + (update[...] - step_two) - relaxed[...]
+        coarse_out[0] = step_two + (update[...] - step_two) - relaxed[...]
 
     @pl.when(is_a)
     def _():
         each(chunks, lambda c: back_hop(c).wait_recv())
-        coarse_v[...] = solved_back[...] - relaxed[...]
-
-    @pl.when(jnp.logical_not(is_pair))
-    def _():
-        coarse_copy().start()
-
-    for side in range(2):
+        coarse_out[0] = solved_back[...] - relaxed[...]
+
+    def add_rows(x, source, start):
+        z = jnp.dot(x, w_v[3, :, own_cols], preferred_element_type=F32)
+        t = jnp.tanh(z + biases[3:4, own_cols])
+        delta = (adjoint_all[source].astype(F32) * h * (1.0 - t * t)).astype(BF16)
+        part = lax.dot_general(x, delta, (((0,), (0,)), ((), ())), preferred_element_type=F32)
+        grad_out[0] = part if start else grad_out[0] + part
+
+    for j in range(1, planes):
+        adjoint_came(j).wait_recv()
+    add_rows(a_own[...], zed, True)
+    for side, source in enumerate((left, right)):
         a_came(side, 1 - side).wait_recv()
-    for j in range(1, planes):
-        for c in range(halves):
-            d_came(j, c).wait_recv()
+        add_rows(a_all[source], source, False)
     for side in range(2):
         a_relayed(side).wait_recv()
-    coarse_copy().wait()
-    for c in range(halves):
-        for copy in own_copies(c):
-            copy.wait()
-
+    add_rows(a_all[across], across, False)
     @pl.when(sends_wide)
     def _():
         each(halves, lambda c: guess_hop(c).wait_send())
@@ -676,11 +648,13 @@
     def _():
         early_hop().wait_send()
 
-    @pl.when(is_a)
+    @pl.when(weight_leaves)
     def _():
         each(PIECES, lambda i: weight_far(i).wait_send())
         bias_hop().wait_send()
 
+    @pl.when(is_a)
+    def _():
         def sent(c):
             far_hop(0, c).wait_send()
             far_hop(1, c).wait_send()
@@ -695,15 +669,12 @@
 
         each(chunks, sent)
 
-    @pl.when(jnp.logical_and(is_pair, row > 0))
-    def _():
-        each(chunks, lambda c: final_row_hop(c).wait_send())
-
     @pl.when(pair_goes_on)
     def _():
         def sent(c):
             below_hop(c).wait_send()
             solved_hop(c).wait_send()
+            final_hop(c, solved).wait_send()
 
         each(chunks, sent)
 
@@ -712,20 +683,18 @@
             a_hop(side, c).wait_send()
         a_relay(side).wait_send()
     for j in range(1, planes):
-        for c in range(halves):
-            d_hop(j, c).wait_send()
-
-
-def finish(new, coarse, a_all, d_all, new_out, coarse_out, grad_out):
-    new_out[...] = new[...]
-    coarse_out[...] = coarse[...]
-    planes, rows, depth = a_all.shape
-    grad_out[0] = lax.dot_general(
-        a_all[...].reshape(planes * rows, depth),
-        d_all[...].reshape(planes * rows, d_all.shape[2]),
-        (((0,), (0,)), ((), ())),
-        preferred_element_type=F32,
-    )
+        adjoint_hop(j).wait_send()
+
+
+def finish(*refs):
+    copies = [
+        pltpu.make_async_copy(src, dst, refs[6].at[i])
+        for i, (src, dst) in enumerate(zip(refs[:3], refs[3:6]))
+    ]
+    for copy in copies:
+        copy.start()
+    for copy in copies:
+        copy.wait()
 
 
 def solution(mesh):
@@ -742,16 +711,15 @@
             pltpu.with_memory_space_constraint(x, pltpu.HBM)
             for x in (inputs, guesses, weights, biases, adjoint)
         ]
-        new, coarse, a_all, d_all = pl.pallas_call(
+        results = pl.pallas_call(
             functools.partial(kernel, blocks),
             out_shape=(
                 jax.ShapeDtypeStruct((1, rows, width), F32),
                 jax.ShapeDtypeStruct((1, rows, width), F32),
-                jax.ShapeDtypeStruct((planes, rows, width), BF16),
-                jax.ShapeDtypeStruct((planes, rows, cols), BF16),
+                jax.ShapeDtypeStruct((1, width, cols), F32),
             ),
             in_specs=[pl.BlockSpec(memory_space=pltpu.HBM)] * 5,
-            out_specs=(anywhere,) * 4,
+            out_specs=(pl.BlockSpec(memory_space=pltpu.VMEM),) * 3,
             scratch_shapes=[
                 pltpu.VMEM((rows, width), F32),
                 pltpu.VMEM((1, rows, width), F32),
@@ -786,11 +754,9 @@
                 pltpu.VMEM((rows, width), BF16),
                 pltpu.VMEM((rows, width), BF16),
                 pltpu.VMEM((rows, width), BF16),
-                whole,
-                whole,
                 pltpu.VMEM((rows, width), BF16),
+                pltpu.VMEM((planes, rows, width), BF16),
                 pltpu.VMEM((planes, rows, cols), BF16),
-                dma((4, halves)),
                 dma((4,)),
                 dma((4,)),
                 dma((2, halves)),
@@ -803,7 +769,7 @@
                 dma((chunks,)),
                 dma((chunks,)),
                 dma((chunks,)),
-                dma((3, chunks)),
+                dma((2, chunks)),
                 dma((chunks,)),
                 dma((2, chunks)),
                 dma((2, chunks)),
@@ -813,34 +779,25 @@
                 dma((2,)),
                 dma((3, halves)),
                 dma((3, halves)),
-                dma((planes - 1, halves)),
-                dma((planes - 1, halves)),
+                dma((planes - 1,)),
+                dma((planes - 1,)),
             ],
             compiler_params=pltpu.CompilerParams(
                 collective_id=0, has_side_effects=True, vmem_limit_bytes=VMEM_MAIN
             ),
             name="mgrit_cycle",
         )(*held)
-        parts = 4
-        slab = pl.BlockSpec((1, rows // parts, width), lambda i: (0, i, 0))
-        return pl.pallas_call(
-            finish,
-            grid=(parts,),
-            out_shape=(
-                jax.ShapeDtypeStruct((1, rows, width), F32),
-                jax.ShapeDtypeStruct((1, rows, width), F32),
-                jax.ShapeDtypeStruct((1, width, cols), F32),
-            ),
-            in_specs=[
-                slab,
-                slab,
-                pl.BlockSpec((planes, rows, width // parts), lambda i: (0, 0, i)),
-                pl.BlockSpec((planes, rows, cols), lambda i: (0, 0, 0)),
-            ],
-            out_specs=(slab, slab, pl.BlockSpec((1, width // parts, cols), lambda i: (0, i, 0))),
-            compiler_params=pltpu.CompilerParams(vmem_limit_bytes=16 * 1024 * 1024),
-            name="results",
-        )(new, coarse, a_all, d_all)
+        return tuple(
+            pl.pallas_call(
+                finish,
+                out_shape=tuple(jax.ShapeDtypeStruct(x.shape, x.dtype) for x in results),
+                in_specs=[pl.BlockSpec(memory_space=pltpu.VMEM)] * 3,
+                out_specs=(anywhere,) * 3,
+                scratch_shapes=[dma((3,))],
+                compiler_params=pltpu.CompilerParams(vmem_limit_bytes=8 * 1024 * 1024),
+                name="results",
+            )(*results)
+        )
 
     return jax.shard_map(
         body,

time: 79.7 us -> 73.1 us (0.917); the launches traced: 78.1 us -> 73 us
  Pallas kernels: 77.5 us -> 72.3 us
    pallas_call x1, Pallas kernels: 75.1 us -> 71 us  [body(): pl.pallas_call(functools.partial(kernel, blocks), out_shape=(jax.ShapeDty...]
    pallas_call x1, Pallas kernels: 2.38 us -> 1.34 us  [body(): pl.pallas_call(finish, out_shape=tuple((jax.ShapeDtypeStruct(x.shape, x.d...]
where the time goes in v5:
time: 73.1 us; the launch traced here: 73 us
  Pallas kernels  72.3 us (99%)
    pallas_call x1, Pallas kernels, body(): pl.pallas_call(functools.partial(kernel, blocks), out_shape=(jax.ShapeDty...  71 us

profile of v5, /device:TPU:31, one launch (start us, length us, event | category | flops | bytes accessed | tf_op | source)
XLA Modules:
  0.0 73.0 jit_solution(15751807671036218563)
XLA Ops:
  0.6 71.0 %mgrit_cycle.1 = (f32[1,128,1024]{2,1,0:T(8,128)S(1)}, f32[1,128,1024]{2,1,0:T(8,128)S(1)}, f32[1,1024,256]{2,1,0:T(8,128)S(1)}) custom-call(f32[128,1024]{1,0:T(8,128)} %inputs_h.1, f32[1,128,1024]{2,1,0:T(8,128)} %guesses_h.1, bf16[4,1024,1024]{2,1,0:T(8,128)(2,1)} %weights.1, f32[4,1024]{1,0:T(4,128)} %biases_h.1, bf16[1,128,1024]{2,1,0:T(8,128)(2,1)} %adjoint_h.1), custom_call_target="tpu_custom_call" | custom-call | tf_op jit(solution)/shard_map/mgrit_cycle/pallas_call | solution.py:714
  71.6 1.3 %results.1 = (f32[1,128,1024]{2,1,0:T(8,128)}, f32[1,128,1024]{2,1,0:T(8,128)}, f32[1,1024,256]{2,1,0:T(8,128)}) custom-call(f32[1,128,1024]{2,1,0:T(8,128)S(1)} %get-tuple-element.6.refs_0_, f32[1,128,1024]{2,1,0:T(8,128)S(1)} %get-tuple-element.7.refs_1_, f32[1,1024,256]{2,1,0:T(8,128)S(1)} %get-tuple-element.8.refs_2_), custom_call_target="tpu_custom_call" | custom-call | tf_op jit(solution)/shard_map/results/pallas_call | solution.py:791

commit v6 on v5

--- a/solution.py
+++ b/solution.py
@@ -36,9 +36,11 @@
     relaxed_in,
     forcing,
     first_v,
+    first_16,
     update,
     level_in,
-    below_in,
+    level_16,
+    below_16,
     below_step,
     own_step,
     solved,
@@ -86,7 +88,7 @@
     adj_send,
     adj_recv,
 ):
-    rows = inputs_h.shape[0]
+    rows, width = inputs_h.shape
     chunks, halves = rows // CHUNK, rows // HALF
     h = 4.0 / (4 * blocks)
     me, zed = lax.axis_index("layer"), lax.axis_index("dp")
@@ -228,8 +230,6 @@
             relaxed_16.at[r], relaxed_in_16.at[r], half_send.at[1, c], half_recv.at[1, c], 1
         )
 
-    is_second = pos == 2
-    relaxed_wide = jnp.logical_not(jnp.logical_or(is_second, is_last))
 
     def await_guess(c):
         @pl.when(takes_wide)
@@ -276,12 +276,12 @@
             source,
         )
 
-    @pl.when(is_second)
+    @pl.when(sends_narrow)
     def _():
         relaxed_16[...] = relaxed[...].astype(BF16)
         each(halves, lambda c: relaxed_hop_16(c).start())
 
-    @pl.when(relaxed_wide)
+    @pl.when(sends_wide)
     def _():
         each(halves, lambda c: relaxed_hop(c).start())
 
@@ -295,17 +295,31 @@
 
     def first_hop(c):
         r = chunk_rows(c)
+        return hop(first_v.at[r], level_in.at[0, r], level_send.at[0, c], level_recv.at[0, c], 1)
+
+    def first_hop_16(c):
+        r = chunk_rows(c)
         return hop(
-            first_v.at[r], level_in.at[slot, r], level_send.at[0, c], level_recv.at[slot, c], 1
+            first_16.at[r], level_16.at[slot, r], level_send.at[0, c], level_recv.at[slot, c], 1
+        )
+
+    def level_came_16(sweep, c):
+        r = chunk_rows(c)
+        return hop(
+            first_16.at[r],
+            level_16.at[sweep, r],
+            level_send.at[0, c],
+            level_recv.at[sweep, c],
+            1,
         )
 
     def below_hop(c):
         r = chunk_rows(c)
-        return hop(first_v.at[r], below_in.at[r], below_send.at[c], below_recv.at[c], 8)
+        return hop(first_16.at[r], below_16.at[r], below_send.at[c], below_recv.at[c], 8)
 
     def far_hop(kind, c):
         r = chunk_rows(c)
-        src, dst = ((first_v, v_in), (update, u_in))[kind]
+        src, dst = ((first_16, v_in), (update, u_in))[kind]
         return hop(src.at[r], dst.at[r], far_send.at[kind, c], far_recv.at[kind, c], 4)
 
     arrivals[3].wait()
@@ -316,12 +330,12 @@
     def forcing_half(c):
         r = half_rows(c)
 
-        @pl.when(pos == 3)
+        @pl.when(takes_narrow)
         def _():
             relaxed_hop_16(c).wait_recv()
             relaxed_in[r, :] = relaxed_in_16[r, :].astype(F32)
 
-        @pl.when(jnp.logical_not(jnp.logical_or(is_first, pos == 3)))
+        @pl.when(takes_wide)
         def _():
             relaxed_hop(c).wait_recv()
 
@@ -352,11 +366,26 @@
     def first_sweep(c):
         r = chunk_rows(c)
 
-        level_hop(0, c, first_v).wait_recv()
+        @pl.when(pos == 3)
+        def _():
+            level_came_16(0, c).wait_recv()
+            level_in[0, r, :] = level_16[0, r, :].astype(F32)
+
+        @pl.when(pos != 3)
+        def _():
+            level_hop(0, c, first_v).wait_recv()
+
         u = level_in[0, r, :]
-        first_v[r, :] = u + (4.0 * h) * act(u, 0) + forcing[r, :]
-
-        @pl.when(jnp.logical_not(is_last))
+        new = u + (4.0 * h) * act(u, 0) + forcing[r, :]
+        narrow = new.astype(BF16)
+        first_16[r, :] = narrow
+        first_v[r, :] = jnp.where(is_c, narrow.astype(F32), new)
+
+        @pl.when(sends_narrow)
+        def _():
+            first_hop_16(c).start()
+
+        @pl.when(pos == 3)
         def _():
             first_hop(c).start()
 
@@ -418,7 +447,12 @@
     def second_sweep(c):
         r = chunk_rows(c)
 
-        @pl.when(jnp.logical_not(is_first))
+        @pl.when(jnp.logical_and(pos == 1, jnp.logical_not(is_first)))
+        def _():
+            level_came_16(1, c).wait_recv()
+            level_in[1, r, :] = level_16[1, r, :].astype(F32)
+
+        @pl.when(pos != 1)
         def _():
             level_hop(1, c, update).wait_recv()
 
@@ -426,7 +460,7 @@
         def _():
             each(chunks // halves, lambda i: far_hop(0, c + i).wait_recv())
             half = half_rows(c // (chunks // halves))
-            v_a = v_in[half, :]
+            v_a = v_in[half, :].astype(F32)
             own_step[half, :] = v_a + (16.0 * h) * act(v_a, 0)
 
         u = level_in[1, r, :]
@@ -458,7 +492,7 @@
         each(PIECES, lambda i: weight_far(i).wait_recv())
         bias_hop().wait_recv()
         each(chunks, lambda c: below_hop(c).wait_recv())
-        u = below_in[...]
+        u = below_16[...].astype(F32)
         below_step[...] = u + (16.0 * h) * act_pair(u)
 
         def solve_both(c):
@@ -523,24 +557,26 @@
             right if side == 0 else left,
         )
 
-    def a_relay(side):
-        r = half_rows(side)
+    def a_relay(side, c):
+        r = half_rows(c)
+        part = pl.ds(side * (width // 2), width // 2)
         source = left if side == 0 else right
         return zhop(
-            a_all.at[source, r],
-            a_all.at[source, r],
-            a_send.at[2, side],
-            a_recv.at[2, side],
+            a_all.at[source, r, part],
+            a_all.at[source, r, part],
+            a_send.at[2 + side, c],
+            a_recv.at[2 + side, c],
             right if side == 0 else left,
         )
 
-    def a_relayed(side):
-        r = half_rows(side)
+    def a_relayed(side, c):
+        r = half_rows(c)
+        part = pl.ds(side * (width // 2), width // 2)
         return zhop(
-            a_own.at[r],
-            a_all.at[across, r],
-            a_send.at[2, side],
-            a_recv.at[2, side],
+            a_own.at[r, part],
+            a_all.at[across, r, part],
+            a_send.at[2 + side, c],
+            a_recv.at[2 + side, c],
             right if side == 0 else left,
         )
 
@@ -577,29 +613,6 @@
         early_send[...] = update[...].astype(BF16)
         early_hop().start()
 
-    for side in range(2):
-        a_came(side, side).wait_recv()
-        a_relay(side).start()
-
-    @pl.when(jnp.logical_not(is_c))
-    def _():
-        @pl.when(me >= 4)
-        def _():
-            early_hop().wait_recv()
-
-        @pl.when(me < 4)
-        def _():
-            early_in[...] = inputs[...].astype(BF16)
-
-        below_step[...] = early_in[...].astype(F32) + (16.0 * h) * act(early_in[...], 0)
-        step_two = below_step[...]
-        coarse_out[0] = step_two + (update[...] - step_two) - relaxed[...]
-
-    @pl.when(is_a)
-    def _():
-        each(chunks, lambda c: back_hop(c).wait_recv())
-        coarse_out[0] = solved_back[...] - relaxed[...]
-
     def add_rows(x, source, start):
         z = jnp.dot(x, w_v[3, :, own_cols], preferred_element_type=F32)
         t = jnp.tanh(z + biases[3:4, own_cols])
@@ -607,15 +620,43 @@
         part = lax.dot_general(x, delta, (((0,), (0,)), ((), ())), preferred_element_type=F32)
         grad_out[0] = part if start else grad_out[0] + part
 
+    def pass_on(c):
+        for side in range(2):
+            a_came(side, c).wait_recv()
+            a_relay(side, c).start()
+
+    pass_on(0)
     for j in range(1, planes):
         adjoint_came(j).wait_recv()
     add_rows(a_own[...], zed, True)
-    for side, source in enumerate((left, right)):
-        a_came(side, 1 - side).wait_recv()
-        add_rows(a_all[source], source, False)
+    pass_on(1)
+
+    @pl.when(jnp.logical_not(is_c))
+    def _():
+        @pl.when(me >= 4)
+        def _():
+            early_hop().wait_recv()
+
+        @pl.when(me < 4)
+        def _():
+            early_in[...] = inputs[...].astype(BF16)
+
+        below_step[...] = early_in[...].astype(F32) + (16.0 * h) * act(early_in[...], 0)
+        step_two = below_step[...]
+        coarse_out[0] = step_two + (update[...] - step_two) - relaxed[...]
+
+    @pl.when(is_a)
+    def _():
+        each(chunks, lambda c: back_hop(c).wait_recv())
+        coarse_out[0] = solved_back[...] - relaxed[...]
+
+    add_rows(a_all[left], left, False)
+    add_rows(a_all[right], right, False)
     for side in range(2):
-        a_relayed(side).wait_recv()
+        for c in range(halves):
+            a_relayed(side, c).wait_recv()
     add_rows(a_all[across], across, False)
+
     @pl.when(sends_wide)
     def _():
         each(halves, lambda c: guess_hop(c).wait_send())
@@ -624,17 +665,21 @@
     def _():
         each(halves, lambda c: guess_hop_16(c).wait_send())
 
-    @pl.when(is_second)
+    @pl.when(sends_narrow)
     def _():
         each(halves, lambda c: relaxed_hop_16(c).wait_send())
 
-    @pl.when(relaxed_wide)
+    @pl.when(sends_wide)
     def _():
         each(halves, lambda c: relaxed_hop(c).wait_send())
 
-    @pl.when(jnp.logical_not(is_last))
+    @pl.when(sends_wide)
     def _():
         each(chunks, lambda c: first_hop(c).wait_send())
+
+    @pl.when(sends_narrow)
+    def _():
+        each(chunks, lambda c: first_hop_16(c).wait_send())
 
     @pl.when(jnp.logical_not(is_c))
     def _():
@@ -681,7 +726,7 @@
     for side in range(2):
         for c in range(halves):
             a_hop(side, c).wait_send()
-        a_relay(side).wait_send()
+            a_relay(side, c).wait_send()
     for j in range(1, planes):
         adjoint_hop(j).wait_send()
 
@@ -732,18 +777,20 @@
                 whole,
                 whole,
                 whole,
+                pltpu.VMEM((rows, width), BF16),
                 whole,
                 pltpu.VMEM((2, rows, width), F32),
-                whole,
-                whole,
-                whole,
-                whole,
-                whole,
-                whole,
-                whole,
-                whole,
-                whole,
-                whole,
+                pltpu.VMEM((2, rows, width), BF16),
+                pltpu.VMEM((rows, width), BF16),
+                whole,
+                whole,
+                whole,
+                whole,
+                whole,
+                whole,
+                whole,
+                whole,
+                pltpu.VMEM((rows, width), BF16),
                 whole,
                 pltpu.VMEM((width, width), BF16),
                 pltpu.VMEM((8, width), F32),
@@ -777,8 +824,8 @@
                 dma((PIECES,)),
                 dma((2,)),
                 dma((2,)),
-                dma((3, halves)),
-                dma((3, halves)),
+                dma((4, halves)),
+                dma((4, halves)),
                 dma((planes - 1,)),
                 dma((planes - 1,)),
             ],

time: 73.1 us -> 71.3 us (0.975)
  Pallas kernels: 72.3 us -> 70.6 us
    pallas_call x1, Pallas kernels: 71 us -> 69.2 us  [body(): pl.pallas_call(functools.partial(kernel, blocks), out_shape=(jax.ShapeDty...]
where the time goes in v6:
time: 71.3 us; the launch traced here: 71.2 us
  Pallas kernels  70.6 us (99%)
    pallas_call x1, Pallas kernels, body(): pl.pallas_call(functools.partial(kernel, blocks), out_shape=(jax.ShapeDty...  69.2 us

profile of v6, /device:TPU:31, one launch (start us, length us, event | category | flops | bytes accessed | tf_op | source)
XLA Modules:
  0.0 71.2 jit_solution(6040302964048732418)
XLA Ops:
  0.6 69.2 %mgrit_cycle.1 = (f32[1,128,1024]{2,1,0:T(8,128)S(1)}, f32[1,128,1024]{2,1,0:T(8,128)S(1)}, f32[1,1024,256]{2,1,0:T(8,128)S(1)}) custom-call(f32[128,1024]{1,0:T(8,128)} %inputs_h.1, f32[1,128,1024]{2,1,0:T(8,128)} %guesses_h.1, bf16[4,1024,1024]{2,1,0:T(8,128)(2,1)} %weights.1, f32[4,1024]{1,0:T(4,128)} %biases_h.1, bf16[1,128,1024]{2,1,0:T(8,128)(2,1)} %adjoint_h.1), custom_call_target="tpu_custom_call" | custom-call | tf_op jit(solution)/shard_map/mgrit_cycle/pallas_call | solution.py:759
  69.9 1.3 %results.1 = (f32[1,128,1024]{2,1,0:T(8,128)}, f32[1,128,1024]{2,1,0:T(8,128)}, f32[1,1024,256]{2,1,0:T(8,128)}) custom-call(f32[1,128,1024]{2,1,0:T(8,128)S(1)} %get-tuple-element.6.refs_0_, f32[1,128,1024]{2,1,0:T(8,128)S(1)} %get-tuple-element.7.refs_1_, f32[1,1024,256]{2,1,0:T(8,128)S(1)} %get-tuple-element.8.refs_2_), custom_call_target="tpu_custom_call" | custom-call | tf_op jit(solution)/shard_map/results/pallas_call | solution.py:838

commit v7 on v6

--- a/solution.py
+++ b/solution.py
@@ -11,7 +11,7 @@
 F32, BF16 = jnp.float32, jnp.bfloat16
 CHUNK = 16
 HALF = 64
-PIECES = 8
+PIECES = 4
 VMEM_MAIN = 40 * 1024 * 1024
 
 
@@ -597,11 +597,21 @@
         t = act(x, 3)
         new_out[0, r, :] = u + h * t
 
-    def final_half(half):
-        each(chunks // halves, lambda c: final_sweep(half * (chunks // halves) + c))
-        block_half(half)
-
-    each(halves, final_half)
+    mixed = jnp.logical_or(is_c, pos == 3)
+
+    def turn(i):
+        block = jnp.where(mixed, lax.rem(i, 2), i // halves)
+        half = jnp.where(mixed, i // 2, lax.rem(i, halves))
+
+        @pl.when(block == 0)
+        def _():
+            each(chunks // halves, lambda c: final_sweep(half * (chunks // halves) + c))
+
+        @pl.when(block == 1)
+        def _():
+            block_half(half)
+
+    each(2 * halves, turn)
 
     def early_hop():
         return hop(early_send, early_in, early_sem.at[0], early_sem.at[1], 4)

time: 71.3 us -> 70.5 us (0.989)
  Pallas kernels: 70.6 us -> 69.8 us
    pallas_call x1, Pallas kernels: 69.2 us -> 68.5 us  [body(): pl.pallas_call(functools.partial(kernel, blocks), out_shape=(jax.ShapeDty...]
where the time goes in v7:
time: 70.5 us; the launch traced here: 70.4 us
  Pallas kernels  69.8 us (99%)
    pallas_call x1, Pallas kernels, body(): pl.pallas_call(functools.partial(kernel, blocks), out_shape=(jax.ShapeDty...  68.5 us

profile of v7, /device:TPU:31, one launch (start us, length us, event | category | flops | bytes accessed | tf_op | source)
XLA Modules:
  0.0 70.4 jit_solution(9684849943037868654)
XLA Ops:
  0.6 68.5 %mgrit_cycle.1 = (f32[1,128,1024]{2,1,0:T(8,128)S(1)}, f32[1,128,1024]{2,1,0:T(8,128)S(1)}, f32[1,1024,256]{2,1,0:T(8,128)S(1)}) custom-call(f32[128,1024]{1,0:T(8,128)} %inputs_h.1, f32[1,128,1024]{2,1,0:T(8,128)} %guesses_h.1, bf16[4,1024,1024]{2,1,0:T(8,128)(2,1)} %weights.1, f32[4,1024]{1,0:T(4,128)} %biases_h.1, bf16[1,128,1024]{2,1,0:T(8,128)(2,1)} %adjoint_h.1), custom_call_target="tpu_custom_call" | custom-call | tf_op jit(solution)/shard_map/mgrit_cycle/pallas_call | solution.py:769
  69.1 1.3 %results.1 = (f32[1,128,1024]{2,1,0:T(8,128)}, f32[1,128,1024]{2,1,0:T(8,128)}, f32[1,1024,256]{2,1,0:T(8,128)}) custom-call(f32[1,128,1024]{2,1,0:T(8,128)S(1)} %get-tuple-element.6.refs_0_, f32[1,128,1024]{2,1,0:T(8,128)S(1)} %get-tuple-element.7.refs_1_, f32[1,1024,256]{2,1,0:T(8,128)S(1)} %get-tuple-element.8.refs_2_), custom_call_target="tpu_custom_call" | custom-call | tf_op jit(solution)/shard_map/results/pallas_call | solution.py:848
